TPU v7x, 32 devices: a whole 2x2x4 slice. The times are simulated.
32 devices in a mesh: section: 2 (over x), tile: 8 (over z, y), member: 2 (over core).
Axes of the slice: x: 2, y: 2, z: 4, core: 2. Of those that a mesh axis runs over, the one named last changes fastest.
Arguments:
- frames: bfloat16 [2, 16, 128, 8, 128], P(None, ('member', 'tile')), parts along dimension 1, may hold values from -6 to 6
- hidden_init: bfloat16 [4, 16, 128, 8, 128], P('section', ('member', 'tile')), parts along dimension 1, may hold values from -0.8984375 to 0.8984375
- memory_init: float32 [4, 16, 128, 8, 128], P('section', ('member', 'tile')), parts along dimension 1, may hold values from -4 to 4
- weights: bfloat16 [4, 512, 2304], P('section'), may hold values from -0.125 to 0.125
- biases: float32 [4, 512], P('section'), may hold values from -3 to 3
Outputs:
- hidden_out: bfloat16 [4, 16, 128, 8, 128], P('section', ('member', 'tile')), parts along dimension 1
- memory_out: float32 [4, 16, 128, 8, 128], P('section', ('member', 'tile')), parts along dimension 1
- gates_out: bfloat16 [2, 4, 16, 512, 8, 128], P(None, 'section', ('member', 'tile')), parts along dimension 2
There are 2 independent parts, one for each index of `member`. A program takes and returns all parts, laid end to end along the dimension named above; an argument that names none is the same for every part. Nothing has to cross between parts.
All inputs are finite; a program needn't handle non-finite values.
Results may differ from a plain program's by a relative error of at most 0.0021.
Values may be sent and summed in bfloat16 or wider, within the bound.
No kernel may reach another device: no remote copies, remote signals or barrier semaphores. Data moves between devices by JAX's collectives and lax.ppermute only.
A program may use at most 128 MiB of HBM per device.

v0:
```python
import jax
import jax.numpy as jnp
from jax import lax
from jax.sharding import PartitionSpec as P

GRID_COLS = 8


def from_behind(block, axis, distance):
    devices = range(lax.axis_size(axis))
    route = [((i - distance) % len(devices), i) for i in devices]
    return lax.ppermute(block, axis, route)


def shifted(shard, axis, by):
    peers = lax.axis_size(axis)
    pairs = [(i, i + by) for i in range(peers) if 0 <= i + by < peers]
    return lax.ppermute(shard, axis, pairs)


def tile_place():
    place = (lax.axis_index("tile") + GRID_COLS + GRID_COLS // 2) % lax.axis_size("tile")
    return (place // GRID_COLS, place % GRID_COLS)


def keep_if(condition, rim):
    return jnp.where(condition, rim, jnp.zeros_like(rim))


def with_rims(source_field):
    row_place, column_place = tile_place()
    grid_rows = lax.axis_size("tile") // GRID_COLS
    upper_rim = from_behind(source_field[:, -1:, :], "tile", GRID_COLS)
    lower_rim = from_behind(source_field[:, :1, :], "tile", -GRID_COLS)
    upper_rim = keep_if(row_place > 0, upper_rim)
    lower_rim = keep_if(row_place < grid_rows - 1, lower_rim)
    heightened = jnp.concatenate([upper_rim, source_field, lower_rim], axis=1)
    left_rim = from_behind(heightened[:, :, -1:], "tile", 1)
    right_rim = from_behind(heightened[:, :, :1], "tile", -1)
    left_rim = keep_if(column_place > 0, left_rim)
    right_rim = keep_if(column_place < GRID_COLS - 1, right_rim)
    return jnp.concatenate([left_rim, heightened, right_rim], axis=2)


def hand_over(hidden_state):
    return shifted(hidden_state, "section", 1)


def advance(stacked, layer_weights, bias_row, memory):
    hidden_count = memory.shape[0]
    height = stacked.shape[1] - 2
    breadth = stacked.shape[2] - 2
    shifted_views = [
        stacked[:, row_offset : row_offset + height, column_offset : column_offset + breadth]
        for row_offset in range(3)
        for column_offset in range(3)
    ]
    patches = jnp.concatenate(shifted_views, axis=0).reshape(9 * stacked.shape[0], height * breadth)
    preact = jnp.dot(layer_weights, patches, preferred_element_type=jnp.float32) + bias_row[:, None]
    preact = preact.reshape(4, hidden_count, height, breadth)
    inflow = jax.nn.sigmoid(preact[0])
    forget = jax.nn.sigmoid(preact[1])
    outflow = jax.nn.sigmoid(preact[2])
    candidate = jnp.tanh(preact[3])
    memory = forget * memory + inflow * candidate
    hidden_state = (outflow * jnp.tanh(memory)).astype(jnp.bfloat16)
    opened = (
        jnp.stack([inflow, forget, outflow, candidate])
        .reshape(4 * hidden_count, height, breadth)
        .astype(jnp.bfloat16)
    )
    return (hidden_state, memory, opened)


def body(frames, hidden_init, memory_init, weights, biases):
    step_count = frames.shape[0]
    layer_count = weights.shape[0]
    channels = frames.shape[2]
    first_section = lax.axis_index("section") == 0
    saved_gates = []
    states = [hidden_init[layer_index, 0] for layer_index in range(layer_count)]
    memories = [memory_init[layer_index, 0] for layer_index in range(layer_count)]
    for moment in range(step_count):
        received = hand_over(states[-1])
        incoming = jnp.where(first_section, frames[moment, 0], received)
        padded = with_rims(jnp.concatenate([incoming] + states, axis=0))
        layer_stacks = [
            padded[layer_index * channels : (layer_index + 2) * channels]
            for layer_index in range(layer_count)
        ]
        fresh_states = []
        fresh_memories = []
        opened_step = []
        for layer_index in range(layer_count):
            hidden_state, memory, opened = advance(
                layer_stacks[layer_index],
                weights[layer_index],
                biases[layer_index],
                memories[layer_index],
            )
            fresh_states.append(hidden_state)
            fresh_memories.append(memory)
            opened_step.append(opened)
        states = fresh_states
        memories = fresh_memories
        saved_gates.append(jnp.stack(opened_step))
    hidden_out = jnp.stack(states)[:, None]
    memory_out = jnp.stack(memories)[:, None]
    gates_out = jnp.stack(saved_gates)[:, :, None]
    return (hidden_out, memory_out, gates_out)


def solution(mesh):
    in_specs = (
        P(None, ("member", "tile"), None, None, None),
        P("section", ("member", "tile"), None, None, None),
        P("section", ("member", "tile"), None, None, None),
        P("section", None, None),
        P("section", None),
    )
    out_specs = (
        P("section", ("member", "tile"), None, None, None),
        P("section", ("member", "tile"), None, None, None),
        P(None, "section", ("member", "tile"), None, None, None),
    )
    return jax.shard_map(body, mesh=mesh, in_specs=in_specs, out_specs=out_specs, check_vma=False)
```

profile of v0, /device:TPU:0, one launch (start us, length us, event | category | flops | bytes accessed | tf_op | source)
XLA Modules:
  0.0 87.2 jit_solution(9434718608333486380)
XLA Ops:
  0.6 1.1 %fusion.94 = (bf16[1,1,128,8,128]{4,3,2,1,0:T(8,128)(2,1)S(1)}, bf16[1,1,128,8,128]{4,3,2,1,0:T(8,128)(2,1)S(1)}) fusion(bf16[2,1,128,8,128]{4,3,2,1,0:T(8,128)(2,1)} %param.6), kind=kLoop, calls=%fused_computation.191 | loop fusion | bytes 1048576 | tf_op jit(solution)/shard_map/slice | solution.py:81
  1.7 0.2 copy.115
  1.9 4.9 %collective-permute-start = (bf16[128,8,128]{0,2,1:T(8,128)(2,1)S(1)}, bf16[128,8,128]{0,2,1:T(8,128)(2,1)S(1)}, u32[]{:S(2)}, u32[]{:S(2)}) collective-permute-start(bf16[128,8,128]{0,2,1:T(8,128)(2,1)S(1)} %bitcast.139), channel_id=1, source_target_pairs={{0,16},{1,17},{2,18},{3,19},{4,20},{5,21},{6,22},{7,23},{8,24},{9,... | collective-permute-start | bytes 786440 | tf_op jit(solution)/shard_map/ppermute | solution.py:18
  6.8 0.2 copy.116
  7.1 1.1 %fusion.93 = (bf16[1,1,128,8,128]{4,3,2,1,0:T(8,128)(2,1)S(1)}, bf16[1,1,128,8,128]{4,3,2,1,0:T(8,128)(2,1)S(1)}) fusion(bf16[2,1,128,8,128]{4,3,2,1,0:T(8,128)(2,1)} %param.5), kind=kLoop, calls=%fused_computation.190 | loop fusion | bytes 1048576 | tf_op jit(solution)/shard_map/slice | solution.py:85
  8.2 0.2 copy.114
  8.4 1.3 %fusion.88 = (f32[1,1,128,8,128]{4,3,2,1,0:T(8,128)S(1)}, f32[1,1,128,8,128]{4,3,2,1,0:T(8,128)S(1)}) fusion(f32[2,1,128,8,128]{4,3,2,1,0:T(8,128)} %param.7), kind=kLoop, calls=%fused_computation.185 | loop fusion | bytes 2097152 | tf_op jit(solution)/shard_map/slice | solution.py:82
  9.7 2.7 %collective-permute-done = bf16[128,8,128]{0,2,1:T(8,128)(2,1)S(1)} collective-permute-done((bf16[128,8,128]{0,2,1:T(8,128)(2,1)S(1)}, bf16[128,8,128]{0,2,1:T(8,128)(2,1)S(1)}, u32[]{:S(2)}, u32[]{:S(2)}) %collective-permute-start) | collective-permute-done | bytes 262176 | tf_op jit(solution)/shard_map/ppermute | solution.py:18
  12.5 0.2 copy.117
  12.8 0.2 copy.118
  13.0 0.9 %copy.113 = bf16[1,1,128,8,128]{2,4,3,1,0:T(8,128)(2,1)} copy(bf16[1,1,128,8,128]{4,3,2,1,0:T(8,128)(2,1)S(1)} %get-tuple-element.92) | data formatting | bytes 524288
  14.1 0.2 pad_maximum_fusion.6
  14.2 4.6 %collective-permute-start.4 = (bf16[384,10,1]{0,1,2:T(8,128)(2,1)S(1)}, bf16[384,10,1]{0,1,2:T(8,128)(2,1)S(1)}, u32[]{:S(2)}, u32[]{:S(2)}) collective-permute-start(bf16[384,10,1]{0,1,2:T(8,128)(2,1)S(1)} %copy.98), channel_id=1, source_target_pairs={{2,0},{4,2},{6,4},{8,6},{10,8},{12,10},{14,12},{0,14},{3,1},{5,3},... | collective-permute-start | bytes 23048 | tf_op jit(solution)/shard_map/ppermute | solution.py:12
  18.9 0.2 fusion.91
  19.0 1.2 %collective-permute-done.4 = bf16[384,10,1]{0,1,2:T(8,128)(2,1)S(1)} collective-permute-done((bf16[384,10,1]{0,1,2:T(8,128)(2,1)S(1)}, bf16[384,10,1]{0,1,2:T(8,128)(2,1)S(1)}, u32[]{:S(2)}, u32[]{:S(2)}) %collective-permute-start.4) | collective-permute-done | bytes 7712 | tf_op jit(solution)/shard_map/ppermute | solution.py:12
  20.3 5.0 %collective-permute-done.3 = bf16[384,10,1]{0,1,2:T(8,128)(2,1)S(1)} collective-permute-done((bf16[384,10,1]{0,1,2:T(8,128)(2,1)S(1)}, bf16[384,10,1]{0,1,2:T(8,128)(2,1)S(1)}, u32[]{:S(2)}, u32[]{:S(2)}) %collective-permute-start.3) | collective-permute-done | bytes 7712 | tf_op jit(solution)/shard_map/ppermute | solution.py:12
  25.3 1.3 %pad_maximum_fusion.4 = (bf16[384,10,129]{0,2,1:T(8,128)(2,1)S(1)}, bf16[384,10,129]{0,2,1:T(8,128)(2,1)S(1)}) fusion(bf16[384,10,1]{0,2,1:T(2,128)(2,1)S(1)} %copy.99, bf16[384,1,128]{0,2,1:T(8,128)(2,1)S(1)} %broadcast_select_fusion.1, bf16[128,8,128]{0,2,1:T(8,128)(2,1)S(1)} %bitcast.143, bf16[128,8,128]{0,2,1:T(8,128)(2,1)S(1)} %bitcast.148, ...), kind=kLoop, calls=%fused_computation.25 | loop fusion | flops 11888640 | bytes 2979840 | tf_op jit(solution)/shard_map/concatenate | solution.py:42
  26.6 0.9 %fusion.89 = (bf16[256,8,128]{0,2,1:T(8,128)(2,1)S(1)}, bf16[256,8,128]{0,2,1:T(8,128)(2,1)S(1)}, bf16[256,8,128]{0,2,1:T(8,128)(2,1)S(1)}, bf16[256,8,128]{0,2,...) fusion(bf16[384,10,129]{0,2,1:T(8,128)(2,1)S(1)} %get-tuple-ele, ...), kind=kLoop, calls=%fused_computation.186 | loop fusion | bytes 12582912 | tf_op jit(solution)/shard_map/slice | solution.py:54
  28.4 0.3 slice-done
  28.6 1.5 %slice-done.1 = s8[4194304]{0:T(1024)(128)(4,1)S(1)} async-done(((s8[4718592]{0:T(1024)(128)(4,1)}), s8[4194304]{0:T(1024)(128)(4,1)S(1)}, s32[]{:S(2)}) %slice-start.1) | async-done | bytes 4194328
  30.1 2.6 %add_bitcast_fusion.3 = f32[512,1024]{0,1:T(8,128)S(1)} fusion(bf16[2304,1024]{0,1:T(8,128)(2,1)S(1)} %constant_dynamic-update-slice_fusion, bf16[2,512,2304]{2,1,0:T(8,128)(2,1)S(1)} %bitcast.210, f32[512]{0:T(512)S(1)} %bitcast.207), kind=kOutput, calls=%fused_computation.14 | convolution fusion | flops 2416443392 | bytes 9177088 | tf_op jit(solution)/shard_map/dot_general | solution.py:59
  32.8 0.5 fusion.78
  33.4 2.6 %add_bitcast_fusion.2 = f32[512,1024]{0,1:T(8,128)S(1)} fusion(bf16[2304,1024]{0,1:T(8,128)(2,1)S(1)} %constant_dynamic-update-slice_fusion.10, bf16[2,512,2304]{2,1,0:T(8,128)(2,1)S(1)} %bitcast.210, f32[512]{0:T(512)S(1)} %bitcast.205), kind=kOutput, calls=%fused_computation.13 | convolution fusion | flops 2416443392 | bytes 9177088 | tf_op jit(solution)/shard_map/dot_general | solution.py:59
  36.1 1.5 %fusion.79 = (bf16[128,1024]{0,1:T(8,128)(2,1)}, bf16[128,1024]{0,1:T(8,128)(2,1)}, f32[128,1024]{0,1:T(8,128)S(1)}, f32[128,1024]{0,1:T(8,128)S(1)}, bf16[128,1024]{0,1:T(8,128)(2,1)}, /*index=5*/f32[128,1024]{0,1:T(8,128)}) fusion(f32[512,1024]{0,1:T(8,128)S(1)} %add_bitcast_fusion.2), kind=kLoop, calls=%fused_computation.142 | loop fusion | flops 1703936 | bytes 4456448 | tf_op jit(solution)/shard_map/convert.13
  37.5 0.2 fusion.69
  37.7 5.1 %collective-permute-start.5 = (bf16[128,8,128]{0,2,1:T(8,128)(2,1)S(1)}, bf16[128,8,128]{0,2,1:T(8,128)(2,1)}, u32[]{:S(2)}, u32[]{:S(2)}) collective-permute-start(bf16[128,8,128]{0,2,1:T(8,128)(2,1)S(1)} %fusion.69), channel_id=1, source_target_pairs={{0,16},{1,17},{2,18},{3,19},{4,20},{5,21},{6,22},{7,23},{8,24},{9,... | collective-permute-start | bytes 786440 | tf_op jit(solution)/shard_map/ppermute | solution.py:18
  42.9 0.1 pad_maximum_fusion.1
  43.0 1.5 %copy.107 = bf16[4,128,8,128]{3,2,1,0:T(8,128)(2,1)} copy(bf16[4,128,8,128]{1,3,2,0:T(8,128)(2,1)S(1)} %pad_maximum_fusion.1) | data formatting | bytes 2097152 | tf_op jit(solution)/shard_map/stack | solution.py:68
  44.5 1.2 %pad_maximum_fusion = bf16[4,128,8,128]{1,3,2,0:T(8,128)(2,1)S(1)} fusion(bf16[1,128,8,128]{1,3,2,0:T(8,128)(2,1)} %bitcast.201, bf16[1,128,8,128]{1,3,2,0:T(8,128)(2,1)} %bitcast.202, bf16[1,128,8,128]{1,3,2,0:T(8,128)(2,1)S(1)} %convert.51, bf16[1,128,8,128]{1,3,2,0:T(8,128)(2,1)} %bitcast.200), kind=kLoop, calls=%fused_computation.20 | loop fusion | flops 1572864 | bytes 2097152 | tf_op jit(solution)/shard_map/stack | solution.py:68
  45.8 1.5 %copy.106 = bf16[4,128,8,128]{3,2,1,0:T(8,128)(2,1)} copy(bf16[4,128,8,128]{1,3,2,0:T(8,128)(2,1)S(1)} %pad_maximum_fusion) | data formatting | bytes 2097152 | tf_op jit(solution)/shard_map/stack | solution.py:68
  47.2 1.3 %fusion.65 = bf16[128,8,128]{0,2,1:T(8,128)(2,1)S(1)} fusion(f32[128,8,128]{0,2,1:T(8,128)} %bitcast.186, f32[128,8,128]{0,2,1:T(8,128)S(1)} %bitcast.159, f32[128,8,128]{0,2,1:T(8,128)S(1)} %bitcast.155, f32[1,1,128,8,128]{2,4,3,1,0:T(8,128)S(1)} %copy.118), kind=kLoop, calls=%fused_computation.113 | loop fusion | flops 524288 | bytes 2359296 | tf_op jit(solution)/shard_map/convert_element_type | solution.py:66
  48.5 1.0 %bitcast_select_fusion.1 = bf16[128,8,128]{0,2,1:T(8,128)(2,1)S(1)} fusion(bf16[128,8,128]{0,2,1:T(8,128)(2,1)} %collective-permute-done.5, bf16[1,1,128,8,128]{2,4,3,1,0:T(8,128)(2,1)} %copy.113, pred[]{:T(512)S(6)} %eq.8), kind=kLoop, calls=%fused_computation.130 | loop fusion | flops 131072 | bytes 786433 | tf_op jit(solution)/shard_map/jit(_where)/select_n | solution.py:85
  49.6 0.2 maximum_bitcast_fusion.1
  50.0 0.2 pad_maximum_fusion.7
  50.2 2.2 %collective-permute-start.8 = (bf16[384,10,1]{0,1,2:T(8,128)(2,1)S(1)}, bf16[384,10,1]{0,1,2:T(8,128)(2,1)S(1)}, u32[]{:S(2)}, u32[]{:S(2)}) collective-permute-start(bf16[384,10,1]{0,1,2:T(8,128)(2,1)S(1)} %copy.102), channel_id=1, source_target_pairs={{14,0},{0,2},{2,4},{4,6},{6,8},{8,10},{10,12},{12,14},{15,1},{1,3}... | collective-permute-start | bytes 23048 | tf_op jit(solution)/shard_map/ppermute | solution.py:12
  52.4 1.2 %collective-permute-done.9 = bf16[384,10,1]{0,1,2:T(8,128)(2,1)S(1)} collective-permute-done((bf16[384,10,1]{0,1,2:T(8,128)(2,1)S(1)}, bf16[384,10,1]{0,1,2:T(8,128)(2,1)S(1)}, u32[]{:S(2)}, u32[]{:S(2)}) %collective-permute-start.9) | collective-permute-done | bytes 7712 | tf_op jit(solution)/shard_map/ppermute | solution.py:12
  53.7 3.1 %collective-permute-done.8 = bf16[384,10,1]{0,1,2:T(8,128)(2,1)S(1)} collective-permute-done((bf16[384,10,1]{0,1,2:T(8,128)(2,1)S(1)}, bf16[384,10,1]{0,1,2:T(8,128)(2,1)S(1)}, u32[]{:S(2)}, u32[]{:S(2)}) %collective-permute-start.8) | collective-permute-done | bytes 7712 | tf_op jit(solution)/shard_map/ppermute | solution.py:12
  56.9 1.3 %pad_maximum_fusion.5 = (bf16[384,10,129]{0,2,1:T(8,128)(2,1)S(1)}, bf16[384,10,129]{0,2,1:T(8,128)(2,1)S(1)}) fusion(bf16[384,10,1]{0,2,1:T(2,128)(2,1)S(1)} %copy.105, bf16[384,1,128]{0,2,1:T(8,128)(2,1)S(1)} %broadcast_select_fusion, bf16[128,8,128]{0,2,1:T(8,128)(2,1)S(1)} %fusion.69, bf16[128,8,128]{0,2,1:T(8,128)(2,1)S(1)} %fusion.65, ...), kind=kLoop, calls=%fused_computation.27 | loop fusion | flops 11888640 | bytes 2979840 | tf_op jit(solution)/shard_map/concatenate | solution.py:42
  58.5 0.4 slice_dynamic-update-slice_fusion.13
  58.8 0.1 slice_dynamic-update-slice_fusion.12
  59.0 0.2 constant_dynamic-update-slice_fusion.20
  59.3 0.4 slice_dynamic-update-slice_fusion.11
  59.9 0.4 slice_dynamic-update-slice_fusion.8
  60.3 0.3 slice-done.2
  60.6 0.3 slice-done.3
  61.0 2.6 %add_bitcast_fusion = f32[512,1024]{0,1:T(8,128)S(1)} fusion(bf16[2304,1024]{0,1:T(8,128)(2,1)S(1)} %bitcast.204, bf16[2,512,2304]{2,1,0:T(8,128)(2,1)S(1)} %bitcast.212, f32[512]{0:T(512)S(1)} %bitcast.208), kind=kOutput, calls=%fused_computation.11 | convolution fusion | flops 2416443392 | bytes 9177088 | tf_op jit(solution)/shard_map/dot_general | solution.py:59
  63.6 1.3 %fusion.81 = (bf16[128,1024]{0,1:T(8,128)(2,1)}, f32[128,1024]{0,1:T(8,128)S(1)}, bf16[128,1024]{0,1:T(8,128)(2,1)}, f32[128,1024]{0,1:T(8,128)S(1)}, f32[128,1024]{0,1:T(8,128)S(1)}) fusion(f32[512,1024]{0,1:T(8,128)S(1)} %add_bitcast_fusion), kind=kLoop, calls=%fused_computation.144 | loop fusion | flops 1572864 | bytes 4194304 | tf_op jit(solution)/shard_map/convert
  64.9 2.6 %add_bitcast_fusion.1 = f32[512,1024]{0,1:T(8,128)S(1)} fusion(bf16[2304,1024]{0,1:T(8,128)(2,1)S(1)} %bitcast.203, bf16[2,512,2304]{2,1,0:T(8,128)(2,1)S(1)} %bitcast.212, f32[512]{0:T(512)S(1)} %bitcast.206), kind=kOutput, calls=%fused_computation.12 | convolution fusion | flops 2416443392 | bytes 9177088 | tf_op jit(solution)/shard_map/dot_general | solution.py:59
  67.6 1.3 %fusion.80 = (bf16[128,1024]{0,1:T(8,128)(2,1)}, f32[128,1024]{0,1:T(8,128)S(1)}, bf16[128,1024]{0,1:T(8,128)(2,1)}, f32[128,1024]{0,1:T(8,128)S(1)}, f32[128,1024]{0,1:T(8,128)S(1)}) fusion(f32[512,1024]{0,1:T(8,128)S(1)} %add_bitcast_fusion.1), kind=kLoop, calls=%fused_computation.143 | loop fusion | flops 1572864 | bytes 4194304 | tf_op jit(solution)/shard_map/convert.4
  68.9 0.8 convert.64
  69.6 0.7 convert.63
  70.4 0.7 convert.60
  71.1 0.7 convert.59
  71.9 1.0 %multiply_convert_fusion = (bf16[1,128,8,128]{1,3,2,0:T(8,128)(2,1)S(1)}, f32[1,128,8,128]{1,3,2,0:T(8,128)}) fusion(f32[1,128,8,128]{1,3,2,0:T(8,128)S(1)} %bitcast.164, f32[1,128,8,128]{1,3,2,0:T(8,128)S(1)} %bitcast.187, f32[1,128,8,128]{1,3,2,0:T(8,128)S(1)} %bitcast.162, f32[1,128,8,128]{1,3,2,0:T(8,128)S(1)} %bitcast.158, ...), kind=kLoop, calls=%fused_computation.119 | loop fusion | flops 786432 | bytes 3932160 | tf_op jit(solution)/shard_map/convert_element_type | solution.py:66
  72.9 1.0 %multiply_convert_fusion.1 = (bf16[1,128,8,128]{1,3,2,0:T(8,128)(2,1)S(1)}, f32[1,128,8,128]{1,3,2,0:T(8,128)}) fusion(f32[1,128,8,128]{1,3,2,0:T(8,128)S(1)} %bitcast.168, f32[1,128,8,128]{1,3,2,0:T(8,128)S(1)} %bitcast.188, f32[1,128,8,128]{1,3,2,0:T(8,128)S(1)} %bitcast.166, f32[1,128,8,128]{1,3,2,0:T(8,128)S(1)} %bitcast.160, ...), kind=kLoop, calls=%fused_computation.120 | loop fusion | flops 786432 | bytes 3932160 | tf_op jit(solution)/shard_map/convert_element_type | solution.py:66
  74.0 1.1 %copy.110 = bf16[2,1,128,8,128]{4,3,2,1,0:T(8,128)(2,1)} copy(bf16[2,1,128,8,128]{2,4,3,0,1:T(8,128)(2,1)S(1)} %maximum_bitcast_fusion.4) | data formatting | bytes 1048576
  75.0 1.3 %maximum_bitcast_fusion.3 = f32[2,1,128,8,128]{2,4,3,0,1:T(8,128)S(1)} fusion(f32[1,128,8,128]{1,3,2,0:T(8,128)} %get-tuple-element.19, f32[1,128,8,128]{1,3,2,0:T(8,128)} %get-tuple-element.17), kind=kLoop, calls=%fused_computation.19 | loop fusion | flops 262144 | bytes 2097152 | tf_op jit(solution)/shard_map/broadcast_in_dim | solution.py:108
  76.3 1.3 %copy.111 = f32[2,1,128,8,128]{4,3,2,1,0:T(8,128)} copy(f32[2,1,128,8,128]{2,4,3,0,1:T(8,128)S(1)} %maximum_bitcast_fusion.3) | data formatting | bytes 2097152
  77.6 1.2 %pad_maximum_fusion.3 = bf16[4,128,8,128]{1,3,2,0:T(8,128)(2,1)S(1)} fusion(bf16[1,128,8,128]{1,3,2,0:T(8,128)(2,1)} %bitcast.194, bf16[1,128,8,128]{1,3,2,0:T(8,128)(2,1)} %convert.64, bf16[1,128,8,128]{1,3,2,0:T(8,128)(2,1)} %convert.63, bf16[1,128,8,128]{1,3,2,0:T(8,128)(2,1)S(1)} %bitcast.193), kind=kLoop, calls=%fused_computation.23 | loop fusion | flops 1572864 | bytes 2097152 | tf_op jit(solution)/shard_map/stack | solution.py:68
  78.9 1.5 %copy.109 = bf16[4,128,8,128]{3,2,1,0:T(8,128)(2,1)} copy(bf16[4,128,8,128]{1,3,2,0:T(8,128)(2,1)S(1)} %pad_maximum_fusion.3) | data formatting | bytes 2097152 | tf_op jit(solution)/shard_map/stack | solution.py:68
  80.3 1.3 %pad_maximum_fusion.2 = bf16[4,128,8,128]{1,3,2,0:T(8,128)(2,1)S(1)} fusion(bf16[1,128,8,128]{1,3,2,0:T(8,128)(2,1)} %bitcast.196, bf16[1,128,8,128]{1,3,2,0:T(8,128)(2,1)} %convert.60, bf16[1,128,8,128]{1,3,2,0:T(8,128)(2,1)} %convert.59, bf16[1,128,8,128]{1,3,2,0:T(8,128)(2,1)} %bitcast.195), kind=kLoop, calls=%fused_computation.22 | loop fusion | flops 1572864 | bytes 2097152 | tf_op jit(solution)/shard_map/stack | solution.py:68
  81.6 1.5 %copy.108 = bf16[4,128,8,128]{3,2,1,0:T(8,128)(2,1)} copy(bf16[4,128,8,128]{1,3,2,0:T(8,128)(2,1)S(1)} %pad_maximum_fusion.2) | data formatting | bytes 2097152 | tf_op jit(solution)/shard_map/stack | solution.py:68
  83.1 1.7 %maximum_bitcast_fusion.2 = bf16[1,2,512,8,128]{4,3,2,1,0:T(8,128)(2,1)S(1)} fusion(bf16[1,512,8,128]{3,2,1,0:T(8,128)(2,1)} %bitcast.171, bf16[1,512,8,128]{3,2,1,0:T(8,128)(2,1)} %bitcast.172), kind=kLoop, calls=%fused_computation.10 | loop fusion | flops 1048576 | bytes 4194304 | tf_op jit(solution)/shard_map/stack | solution.py:109
  84.8 2.4 %maximum_bitcast_fusion = bf16[2,2,1,512,8,128]{5,4,3,2,1,0:T(8,128)(2,1)} fusion(bf16[1,2,512,8,128]{4,3,2,1,0:T(8,128)(2,1)S(1)} %maximum_bitcast_fusion.2, bf16[1,2,512,8,128]{4,3,2,1,0:T(8,128)(2,1)S(1)} %maximum_bitcast_fusion.1), kind=kLoop, calls=%fused_computation | loop fusion | flops 2097152 | bytes 8388608
  (91 shorter events, 2.1 us)
Async XLA Ops:
  0.6 11.8 %copy-start.11 = (f32[2,512]{1,0:T(2,128)S(1)}, f32[2,512]{1,0:T(2,128)}, u32[]{:S(2)}) copy-start(f32[2,512]{1,0:T(2,128)} %param.9) | copy-start | bytes 12292
  1.9 10.4 %collective-permute-start = (bf16[128,8,128]{0,2,1:T(8,128)(2,1)S(1)}, bf16[128,8,128]{0,2,1:T(8,128)(2,1)S(1)}, u32[]{:S(2)}, u32[]{:S(2)}) collective-permute-start(bf16[128,8,128]{0,2,1:T(8,128)(2,1)S(1)} %bitcast.139), channel_id=1, source_target_pairs={{0,16},{1,17},{2,18},{3,19},{4,20},{5,21},{6,22},{7,23},{8,24},{9,... | collective-permute-start | bytes 786440 | tf_op jit(solution)/shard_map/ppermute | solution.py:18
  12.4 1.5 %collective-permute-start.2 = (bf16[384,1,128]{0,2,1:T(8,128)(2,1)S(1)}, bf16[384,1,128]{0,2,1:T(8,128)(2,1)S(1)}, u32[]{:S(2)}, u32[]{:S(2)}) collective-permute-start(bf16[384,1,128]{0,2,1:T(8,128)(2,1)S(1)} %get-tuple-element.91), channel_id=1, source_target_pairs={{0,0},{2,2},{4,4},{6,6},{8,8},{10,10},{12,12},{14,14},{1,1},{3,3},... | collective-permute-start | bytes 294920 | tf_op jit(solution)/shard_map/ppermute | solution.py:12
  12.8 24.8 %copy-start.6 = (f32[1,1,128,8,128]{2,4,3,1,0:T(8,128)}, f32[1,1,128,8,128]{2,4,3,1,0:T(8,128)S(1)}, u32[]{:S(2)}) copy-start(f32[1,1,128,8,128]{2,4,3,1,0:T(8,128)S(1)} %copy.117) | copy-start | bytes 1572868
  13.0 34.2 %copy-start.4 = (f32[1,1,128,8,128]{2,4,3,1,0:T(8,128)}, f32[1,1,128,8,128]{2,4,3,1,0:T(8,128)S(1)}, u32[]{:S(2)}) copy-start(f32[1,1,128,8,128]{2,4,3,1,0:T(8,128)S(1)} %copy.118) | copy-start | bytes 1572868
  14.2 6.0 %collective-permute-start.4 = (bf16[384,10,1]{0,1,2:T(8,128)(2,1)S(1)}, bf16[384,10,1]{0,1,2:T(8,128)(2,1)S(1)}, u32[]{:S(2)}, u32[]{:S(2)}) collective-permute-start(bf16[384,10,1]{0,1,2:T(8,128)(2,1)S(1)} %copy.98), channel_id=1, source_target_pairs={{2,0},{4,2},{6,4},{8,6},{10,8},{12,10},{14,12},{0,14},{3,1},{5,3},... | collective-permute-start | bytes 23048 | tf_op jit(solution)/shard_map/ppermute | solution.py:12
  18.8 6.4 %collective-permute-start.3 = (bf16[384,10,1]{0,1,2:T(8,128)(2,1)S(1)}, bf16[384,10,1]{0,1,2:T(8,128)(2,1)S(1)}, u32[]{:S(2)}, u32[]{:S(2)}) collective-permute-start(bf16[384,10,1]{0,1,2:T(8,128)(2,1)S(1)} %copy.96), channel_id=1, source_target_pairs={{14,0},{0,2},{2,4},{4,6},{6,8},{8,10},{10,12},{12,14},{15,1},{1,3}... | collective-permute-start | bytes 23048 | tf_op jit(solution)/shard_map/ppermute | solution.py:12
  27.6 1.0 %slice-start = ((s8[4718592]{0:T(1024)(128)(4,1)}), s8[524288]{0:T(1024)(128)(4,1)S(1)}, s32[]{:S(2)}) async-start(s8[4718592]{0:T(1024)(128)(4,1)} %bitcast.209), calls=%async_computation | async-start | bytes 1048576
  27.9 2.2 %slice-start.1 = ((s8[4718592]{0:T(1024)(128)(4,1)}), s8[4194304]{0:T(1024)(128)(4,1)S(1)}, s32[]{:S(2)}) async-start(s8[4718592]{0:T(1024)(128)(4,1)} %bitcast.209), calls=%async_computation.1 | async-start | bytes 8388608
  33.2 4.3 %copy-start = (f32[128,1024]{0,1:T(8,128)}, f32[128,1024]{0,1:T(8,128)S(1)}, u32[]{:S(2)}) copy-start(f32[128,1024]{0,1:T(8,128)S(1)} %get-tuple-element.28) | copy-start | bytes 1572868
  37.5 9.7 %copy-start.2 = (f32[128,1024]{0,1:T(8,128)}, f32[128,1024]{0,1:T(8,128)S(1)}, u32[]{:S(2)}) copy-start(f32[128,1024]{0,1:T(8,128)S(1)} %get-tuple-element.22) | copy-start | bytes 1572868
  37.7 10.8 %collective-permute-start.5 = (bf16[128,8,128]{0,2,1:T(8,128)(2,1)S(1)}, bf16[128,8,128]{0,2,1:T(8,128)(2,1)}, u32[]{:S(2)}, u32[]{:S(2)}) collective-permute-start(bf16[128,8,128]{0,2,1:T(8,128)(2,1)S(1)} %fusion.69), channel_id=1, source_target_pairs={{0,16},{1,17},{2,18},{3,19},{4,20},{5,21},{6,22},{7,23},{8,24},{9,... | collective-permute-start | bytes 786440 | tf_op jit(solution)/shard_map/ppermute | solution.py:18
  47.2 2.4 %copy-start.8 = (bf16[4,128,8,128]{3,2,1,0:T(8,128)(2,1)S(1)}, bf16[4,128,8,128]{3,2,1,0:T(8,128)(2,1)}, u32[]{:S(2)}) copy-start(bf16[4,128,8,128]{3,2,1,0:T(8,128)(2,1)} %copy.107) | copy-start | bytes 3145732
  47.2 2.4 %copy-start.9 = (bf16[4,128,8,128]{3,2,1,0:T(8,128)(2,1)S(1)}, bf16[4,128,8,128]{3,2,1,0:T(8,128)(2,1)}, u32[]{:S(2)}) copy-start(bf16[4,128,8,128]{3,2,1,0:T(8,128)(2,1)} %copy.106) | copy-start | bytes 3145732
  49.6 0.3 collective-permute-start.7
  49.8 0.1 collective-permute-start.6
  49.9 3.7 %collective-permute-start.9 = (bf16[384,10,1]{0,1,2:T(8,128)(2,1)S(1)}, bf16[384,10,1]{0,1,2:T(8,128)(2,1)S(1)}, u32[]{:S(2)}, u32[]{:S(2)}) collective-permute-start(bf16[384,10,1]{0,1,2:T(8,128)(2,1)S(1)} %copy.104), channel_id=1, source_target_pairs={{2,0},{4,2},{6,4},{8,6},{10,8},{12,10},{14,12},{0,14},{3,1},{5,3},... | collective-permute-start | bytes 23048 | tf_op jit(solution)/shard_map/ppermute | solution.py:12
  50.2 6.6 %collective-permute-start.8 = (bf16[384,10,1]{0,1,2:T(8,128)(2,1)S(1)}, bf16[384,10,1]{0,1,2:T(8,128)(2,1)S(1)}, u32[]{:S(2)}, u32[]{:S(2)}) collective-permute-start(bf16[384,10,1]{0,1,2:T(8,128)(2,1)S(1)} %copy.102), channel_id=1, source_target_pairs={{14,0},{0,2},{2,4},{4,6},{6,8},{8,10},{10,12},{12,14},{15,1},{1,3}... | collective-permute-start | bytes 23048 | tf_op jit(solution)/shard_map/ppermute | solution.py:12
  58.5 2.2 %slice-start.2 = ((s8[4718592]{0:T(1024)(128)(4,1)}), s8[4194304]{0:T(1024)(128)(4,1)S(1)}, s32[]{:S(2)}) async-start(s8[4718592]{0:T(1024)(128)(4,1)} %bitcast.211), calls=%async_computation.2 | async-start | bytes 8388608
  59.3 1.7 %slice-start.3 = ((s8[4718592]{0:T(1024)(128)(4,1)}), s8[524288]{0:T(1024)(128)(4,1)S(1)}, s32[]{:S(2)}) async-start(s8[4718592]{0:T(1024)(128)(4,1)} %bitcast.211), calls=%async_computation.3 | async-start | bytes 1048576
  67.5 4.3 %copy-start.1 = (f32[128,1024]{0,1:T(8,128)S(1)}, f32[128,1024]{0,1:T(8,128)}, u32[]{:S(2)}) copy-start(f32[128,1024]{0,1:T(8,128)} %copy-done) | copy-start | bytes 1572868
  67.5 4.3 %copy-start.7 = (f32[1,1,128,8,128]{2,4,3,1,0:T(8,128)S(1)}, f32[1,1,128,8,128]{2,4,3,1,0:T(8,128)}, u32[]{:S(2)}) copy-start(f32[1,1,128,8,128]{2,4,3,1,0:T(8,128)} %copy-done.6) | copy-start | bytes 1572868
  67.6 5.3 %copy-start.3 = (f32[128,1024]{0,1:T(8,128)S(1)}, f32[128,1024]{0,1:T(8,128)}, u32[]{:S(2)}) copy-start(f32[128,1024]{0,1:T(8,128)} %copy-done.2) | copy-start | bytes 1572868
  67.6 5.3 %copy-start.5 = (f32[1,1,128,8,128]{2,4,3,1,0:T(8,128)S(1)}, f32[1,1,128,8,128]{2,4,3,1,0:T(8,128)}, u32[]{:S(2)}) copy-start(f32[1,1,128,8,128]{2,4,3,1,0:T(8,128)} %copy-done.4) | copy-start | bytes 1572868
  73.9 3.7 %copy-start.10 = (bf16[128,1024]{0,1:T(8,128)(2,1)S(1)}, bf16[128,1024]{0,1:T(8,128)(2,1)}, u32[]{:S(2)}) copy-start(bf16[128,1024]{0,1:T(8,128)(2,1)} %get-tuple-element.37) | copy-start | bytes 786436
  (1 other events, 0.0 us)
where the time goes:
time: 87.6 us; the launch traced here: 87.2 us
  other arithmetic  24.9 us (28%)
  local copies, waits for them, and re-layouts  20.1 us (23%)
  starting transfers between devices  16.9 us (19%)
  waiting for transfers between devices  13.3 us (15%)
  matrix products  10.5 us (12%)
  between operations  1.45 us (2%)
    ppermute x8, waiting for transfers between devices, from_behind(): return lax.ppermute(block, axis, route)  10.6 us
    dot_general x4, matrix products, advance(): jnp.dot(layer_weights, patches, preferred_element_type=jnp.float32)  10.5 us
    ppermute x2, starting transfers between devices, shifted(): return lax.ppermute(shard, axis, pairs)  9.99 us
    unnamed x67, local copies, waits for them, and re-layouts  9.28 us
    another operation x10, other arithmetic  7.61 us
    ppermute x8, starting transfers between devices, from_behind(): return lax.ppermute(block, axis, route)  6.96 us
    another operation x4, local copies, waits for them, and re-layouts, advance(): jnp.stack([inflow, forget, outflow, candidate])  5.82 us
    another operation x4, other arithmetic, advance(): jnp.stack([inflow, forget, outflow, candidate])  3.93 us
  transfers between devices with their start and end apart: 10, of which 5 were waited for; matrix products, arithmetic and copies ran while one was open for 12% of the time, Pallas kernels for 0%

commit v1 on v0

--- a/solution.py
+++ b/solution.py
@@ -1,9 +1,482 @@
 import jax
 import jax.numpy as jnp
 from jax import lax
+from jax.experimental import pallas as pl
+from jax.experimental.pallas import tpu as pltpu
 from jax.sharding import PartitionSpec as P
 
 GRID_COLS = 8
+LANES = 128
+
+bf16 = jnp.bfloat16
+f32 = jnp.float32
+VMEM = pl.BlockSpec(memory_space=pltpu.VMEM)
+ANY = pl.BlockSpec(memory_space=pl.ANY)
+EDGE = 16
+
+
+def iota(shape, dim):
+    return lax.broadcasted_iota(jnp.int32, shape, dim)
+
+
+def params():
+    return pltpu.CompilerParams(vmem_limit_bytes=24 * 2**20)
+
+
+def in_vmem(array):
+    return pltpu.with_memory_space_constraint(array, pltpu.VMEM)
+
+
+def tile_place():
+    return (lax.axis_index("tile") + GRID_COLS + GRID_COLS // 2) % lax.axis_size("tile")
+
+
+def swap_pairs(parity):
+    count = lax.axis_size("tile")
+    index = {(k + GRID_COLS + GRID_COLS // 2) % count: k for k in range(count)}
+    pairs = []
+    for place in range(count - 1):
+        if place % 2 == parity and place % GRID_COLS != GRID_COLS - 1:
+            pairs += [(index[place], index[place + 1]), (index[place + 1], index[place])]
+    return pairs
+
+
+def swap_matrix(rows, block, to_rows_first):
+    size = rows * block
+    m = iota((size, size), 0)
+    n = iota((size, size), 1)
+    if to_rows_first:
+        m, n = n, m
+    return jnp.where((m // rows == n % block) & (m % rows == n // block), 1.0, 0.0).astype(bf16)
+
+
+def prep_kernel(frames, hidden, memory, bias, xt, first_edges, second_edges, cells, wide_bias, raw, sems):
+    layers, flat, _ = hidden.shape
+    rows = xt.shape[0]
+    channels = flat // rows
+    copies = [
+        pltpu.make_async_copy(hidden, raw.at[pl.ds(0, layers)], sems.at[0]),
+        pltpu.make_async_copy(frames, raw.at[pl.ds(layers, frames.shape[0])], sems.at[1]),
+        pltpu.make_async_copy(memory, cells, sems.at[2]),
+    ]
+    for copy in copies:
+        copy.start()
+    gates = wide_bias.shape[1]
+    for layer in range(layers):
+        for q in range(4):
+            part = bias[layer : layer + 1, q * channels : (q + 1) * channels]
+            part = jnp.broadcast_to(part, (channels, channels)).T
+            wide_bias[layer, q * channels : (q + 1) * channels] = part * (0.5 if q < 3 else 1.0)
+    block = 256 // rows
+    order = swap_matrix(rows, block, True)
+    count = raw.shape[0]
+    width = rows * LANES
+    m = iota((width, LANES), 0)
+    lane = iota((width, LANES), 1)
+    near = lane // rows
+    to_right = (lane < 2 * rows) & (m == (lane % rows) * LANES + (LANES - 2) + near)
+    to_left = (lane < 2 * rows) & (m == (lane % rows) * LANES + 1 - near)
+    select = jnp.concatenate(
+        [jnp.where(to_right, 1.0, 0.0).astype(bf16), jnp.where(to_left, 1.0, 0.0).astype(bf16)], axis=1
+    )
+    copies[0].wait()
+    copies[1].wait()
+    for pair in range(0, count, 2):
+        for group in range(channels // block):
+            part = pl.ds(group * 256, 256)
+            both = jnp.concatenate([raw[pair, part], raw[pair + 1, part]], axis=1)
+            out = jnp.dot(order, both, preferred_element_type=f32).astype(bf16)
+            for r in range(rows):
+                for k in range(2):
+                    at = (pair + k) * channels + group * block
+                    xt[r, at : at + block] = out[r * block : (r + 1) * block, k * LANES : (k + 1) * LANES]
+    wide = jnp.concatenate([xt[r] for r in range(rows)], axis=1)
+    edges = jnp.dot(wide, select, preferred_element_type=f32)
+    right = jnp.zeros((channels, LANES), f32)
+    left = jnp.zeros((channels, LANES), f32)
+    for k in range(count):
+        part = edges[k * channels : (k + 1) * channels]
+        right += pltpu.roll(part[:, :LANES], k * EDGE, 1)
+        left += pltpu.roll(part[:, LANES:], k * EDGE, 1)
+    copies[2].wait()
+    lane = iota((channels, LANES), 1)
+    cell_right = jnp.zeros((channels, LANES), f32)
+    cell_left = jnp.zeros((channels, LANES), f32)
+    for layer in range(layers):
+        for r in range(rows):
+            row = cells[layer, pl.ds(r, channels, stride=rows), :]
+            to = (count + layer) * EDGE + r
+            cell_right = jnp.where(lane == to, pltpu.roll(row, (to + 1) % LANES, 1), cell_right)
+            cell_left = jnp.where(lane == to, pltpu.roll(row, to, 1), cell_left)
+
+    def split(value):
+        high = value.astype(bf16)
+        low = (value - high.astype(f32)).astype(bf16)
+        return high.astype(f32) + pltpu.roll(low.astype(f32), rows, 1)
+
+    right = (right + split(cell_right)).astype(bf16)
+    left = (left + split(cell_left)).astype(bf16)
+    even = tile_place() % 2 == 0
+    first_edges[...] = jnp.where(even, right, left)
+    second_edges[...] = jnp.where(even, left, right)
+
+
+def pick(lane, start, size, value, rest):
+    return jnp.where((lane >= start) & (lane < start + size), value, rest)
+
+
+def edge_kernel(xt, first_own, second_own, first_got, second_got, packet, packed, next_edge, cell_edge):
+    rows = xt.shape[0]
+    channels = packet.shape[1]
+    layers = cell_edge.shape[0]
+    even = tile_place() % 2 == 0
+    own_right = jnp.where(even, first_own[...], second_own[...]).astype(f32)
+    own_left = jnp.where(even, second_own[...], first_own[...]).astype(f32)
+    from_left = jnp.where(even, second_got[...], first_got[...]).astype(f32)
+    from_right = jnp.where(even, first_got[...], second_got[...]).astype(f32)
+    lane = iota((channels, LANES), 1)
+
+    def turned(value, by):
+        return pltpu.roll(value, by % LANES, 1)
+
+    def columns(k):
+        base = -k * EDGE
+        out = jnp.zeros((channels, LANES), f32)
+        out = pick(lane, 0, rows, turned(from_left, base), out)
+        out = pick(lane, rows, rows, turned(own_right, base), out)
+        out = pick(lane, 2 * rows, rows, turned(from_left, base + rows), out)
+        out = pick(lane, 3 * rows, rows, turned(from_right, base + 2 * rows), out)
+        out = pick(lane, 4 * rows, rows, turned(own_left, base + 3 * rows), out)
+        out = pick(lane, 5 * rows, rows, turned(from_right, base + 5 * rows), out)
+        return out.astype(bf16)
+
+    last = layers - 1
+    for k in range(layers + 1):
+        packed[k] = columns(k)
+    next_edge[...] = columns(layers + 1)
+    packet[rows] = packed[last]
+    for r in range(rows):
+        packet[r] = xt[r, last * channels : (last + 1) * channels]
+    for layer in range(layers):
+        base = -(layers + 2 + layer) * EDGE
+        a = turned(from_left, base)
+        b = turned(from_right, base)
+        a = a + turned(a, -rows)
+        b = b + turned(b, -rows)
+        cell_edge[layer] = jnp.where(lane < rows, a, turned(b, rows))
+
+
+def cell_step(pre, bias, memory):
+    channels = memory.shape[0]
+
+    def gate(q):
+        part = slice(q * channels, (q + 1) * channels)
+        if q == 3:
+            return jnp.tanh(pre[part] + bias[part])
+        return jnp.tanh(pre[part] * 0.5 + bias[part]) * 0.5 + 0.5
+
+    inflow, forget, outflow, candidate = gate(0), gate(1), gate(2), gate(3)
+    memory = forget * memory + inflow * candidate
+    hidden = (outflow * jnp.tanh(memory)).astype(bf16)
+    return (inflow, forget, outflow, candidate), memory, hidden
+
+
+def run_layer(sources, edge_columns, weights, bias, memory_of, memory_out, hidden_rows, cell_edge, gates_at, scratch):
+    shifted, gate_rows, gate_tiles, sems = scratch
+    rows = shifted.shape[1] - 2
+    channels = shifted.shape[2] // 2
+    lane = iota((channels, LANES), 1)
+    blank = jnp.zeros((2 * channels, LANES), bf16)
+    for b in range(3):
+        shifted[b, 0] = blank
+        shifted[b, rows + 1] = blank
+    for k in range(2):
+        part = slice(k * channels, (k + 1) * channels)
+        for r in range(rows):
+            x = sources[k](r)
+            before = pltpu.roll(edge_columns[k], LANES - 2 * rows - r, 1)
+            after = pltpu.roll(edge_columns[k], LANES - 1 - 3 * rows - r, 1)
+            shifted[1, r + 1, part] = x
+            shifted[0, r + 1, part] = jnp.where(lane == 0, before, pltpu.roll(x, 1, 1))
+            shifted[2, r + 1, part] = jnp.where(lane == LANES - 1, after, pltpu.roll(x, LANES - 1, 1))
+    for j in range(rows // 2):
+        patches = jnp.concatenate(
+            [
+                jnp.concatenate([shifted[b, 2 * j + a], shifted[b, 2 * j + a + 1]], axis=1)
+                for a in range(3)
+                for b in range(3)
+            ],
+            axis=0,
+        )
+        total = jnp.dot(weights, patches, preferred_element_type=f32)
+        for k in range(2):
+            r = 2 * j + k
+            at = pl.ds(r, channels, stride=rows)
+            gates, memory, hidden = cell_step(total[:, k * LANES : (k + 1) * LANES], bias, memory_of(at))
+            memory_out[at, :] = memory
+            hidden_rows[r] = hidden
+            for q in range(4):
+                gate_rows[r, q * channels : (q + 1) * channels] = gates[q].astype(bf16)
+    if cell_edge is not None:
+        wide = jnp.concatenate(edge_columns, axis=0)
+        wide_lane = iota((2 * channels, LANES), 1)
+        parts = []
+        for a in range(3):
+            row = wide_lane % rows + (a - 1)
+            for b in range(3):
+                moved = pltpu.roll(wide, (-2 * rows * b - (a - 1)) % LANES, 1)
+                parts.append(jnp.where((row >= 0) & (row < rows), moved, jnp.zeros_like(moved)))
+        total = jnp.dot(weights, jnp.concatenate(parts, axis=0), preferred_element_type=f32)
+        _, _, hidden = cell_step(total, bias, cell_edge)
+        place = tile_place() % GRID_COLS
+        inside = ((lane < rows) & (place > 0)) | ((lane >= rows) & (lane < 2 * rows) & (place < GRID_COLS - 1))
+        hidden = jnp.where(inside, hidden, jnp.zeros_like(hidden))
+        hidden_rows[rows] = pltpu.roll(hidden, 2 * rows, 1)
+    copies = []
+    for first in range(0, gate_rows.shape[1] * rows, 512):
+        restore(gate_rows, gate_tiles, first)
+        part = pl.ds(first, 512)
+        copy = pltpu.make_async_copy(gate_tiles.at[part], gates_at.at[part], sems.at[first // 512])
+        copy.start()
+        copies.append(copy)
+    return copies
+
+
+def restore(source, target, first):
+    rows = source.shape[0]
+    block = 256 // rows
+    order = swap_matrix(rows, block, False)
+    both = []
+    for at in (first // rows, first // rows + block):
+        both.append(jnp.concatenate([source[r, at : at + block] for r in range(rows)], axis=0))
+    out = jnp.dot(order, jnp.concatenate(both, axis=1), preferred_element_type=f32).astype(bf16)
+    target[first : first + 256] = out[:, :LANES]
+    target[first + 256 : first + 512] = out[:, LANES:]
+
+
+def finish(copies):
+    for copy in copies:
+        copy.wait()
+
+
+def part_of(ref, k, channels):
+    def load(r):
+        return ref[r, k * channels : (k + 1) * channels]
+
+    return load
+
+
+def either(condition, one, other):
+    def load(r):
+        return jnp.where(condition, one(r), other(r))
+
+    return load
+
+
+def whole(ref):
+    return lambda r: ref[r]
+
+
+def first_last_layer(xt, packed, weights, bias, cells, cell_edge, hidden, memory, gates, *scratch):
+    layer = weights.shape[0] - 1
+    copies = run_layer(
+        (part_of(xt, layer - 1, packed.shape[1]), part_of(xt, layer, packed.shape[1])),
+        (packed[layer - 1], packed[layer]),
+        weights[layer],
+        bias[layer],
+        lambda at: cells[layer, at, :],
+        memory,
+        hidden,
+        cell_edge[layer],
+        gates.at[0, layer],
+        scratch,
+    )
+    finish(copies)
+
+
+def first_first_layer(
+    xt, packet, packed, weights, bias, cells, cell_edge, _, hidden, memory, gates, *scratch
+):
+    first = lax.axis_index("section") == 0
+    layers = weights.shape[0]
+    rows = packet.shape[0] - 1
+    copies = run_layer(
+        (either(first, part_of(xt, layers, packet.shape[1]), whole(packet)), part_of(xt, 0, packet.shape[1])),
+        (jnp.where(first, packed[layers], packet[rows]), packed[0]),
+        weights[0],
+        bias[0],
+        lambda at: cells[0, at, :],
+        memory,
+        hidden,
+        cell_edge[0],
+        gates.at[0, 0],
+        scratch,
+    )
+    finish(copies)
+
+
+def close_layer(layer, scratch, hidden_rows, hidden_tiles, memory_tiles, hidden_out, memory_out, sems):
+    flat = hidden_tiles.shape[0]
+    saves = [pltpu.make_async_copy(memory_tiles, memory_out.at[layer], sems.at[0])]
+    saves[0].start()
+    for first in range(0, flat, 512):
+        restore(hidden_rows, hidden_tiles, first)
+    saves.append(pltpu.make_async_copy(hidden_tiles, hidden_out.at[layer], sems.at[1]))
+    saves[1].start()
+    return saves
+
+
+def second_last_layer(before, last, weights, bias, memory, _, gates, hidden_out, memory_out, *scratch):
+    *scratch, hidden_rows, hidden_tiles, memory_tiles, sems = scratch
+    layer = weights.shape[0] - 1
+    rows = before.shape[0] - 1
+    copies = run_layer(
+        (whole(before), whole(last)),
+        (before[rows], last[rows]),
+        weights[layer],
+        bias[layer],
+        lambda at: memory[at, :],
+        memory_tiles,
+        hidden_rows,
+        None,
+        gates.at[1, layer],
+        scratch,
+    )
+    copies += close_layer(
+        layer, scratch, hidden_rows, hidden_tiles, memory_tiles, hidden_out, memory_out, sems
+    )
+    finish(copies)
+
+
+def second_first_layer(
+    xt, packet, next_edge, last, weights, bias, memory, _, __, ___, gates, hidden_out, memory_out, *scratch
+):
+    *scratch, hidden_rows, hidden_tiles, memory_tiles, sems = scratch
+    first = lax.axis_index("section") == 0
+    rows = packet.shape[0] - 1
+    frame = xt.shape[1] // packet.shape[1] - 1
+    copies = run_layer(
+        (either(first, part_of(xt, frame, packet.shape[1]), whole(packet)), whole(last)),
+        (jnp.where(first, next_edge[...], packet[rows]), last[rows]),
+        weights[0],
+        bias[0],
+        lambda at: memory[at, :],
+        memory_tiles,
+        hidden_rows,
+        None,
+        gates.at[1, 0],
+        scratch,
+    )
+    copies += close_layer(
+        0, scratch, hidden_rows, hidden_tiles, memory_tiles, hidden_out, memory_out, sems
+    )
+    finish(copies)
+
+
+def wavefront(frames, hidden_init, memory_init, weights, biases):
+    steps, _, channels, rows, _ = frames.shape
+    layers, gate_count, _ = weights.shape
+    flat = channels * rows
+    frames = frames.reshape(steps, flat, LANES)
+    hidden_init = hidden_init.reshape(layers, flat, LANES)
+    memory_init = memory_init.reshape(layers, flat, LANES)
+    plane = (channels, LANES)
+    sections = lax.axis_size("section")
+    ahead = [(i, i + 1) for i in range(sections - 1)]
+
+    def call(kernel, ins, outs, scratch=(), aliases=None, places=None):
+        return pl.pallas_call(
+            kernel,
+            in_specs=places[0] if places else [VMEM] * len(ins),
+            out_specs=places[1] if places else [VMEM] * len(outs),
+            out_shape=outs,
+            scratch_shapes=list(scratch),
+            input_output_aliases=aliases or {},
+            compiler_params=params(),
+        )(*ins)
+
+    xt, first_edges, second_edges, cells, wide_bias = call(
+        prep_kernel,
+        (frames, hidden_init, memory_init, biases),
+        [
+            pltpu.VMEM((rows, (layers + steps) * channels, LANES), bf16),
+            pltpu.VMEM(plane, bf16),
+            pltpu.VMEM(plane, bf16),
+            pltpu.VMEM((layers, flat, LANES), f32),
+            pltpu.VMEM((layers, gate_count, LANES), f32),
+        ],
+        [pltpu.VMEM((layers + steps, flat, LANES), bf16), pltpu.SemaphoreType.DMA((3,))],
+        places=([ANY, ANY, ANY, VMEM], [VMEM] * 5),
+    )
+    first_got = in_vmem(lax.ppermute(first_edges, "tile", swap_pairs(0)))
+    second_got = in_vmem(lax.ppermute(second_edges, "tile", swap_pairs(1)))
+    packet, packed, next_edge, cell_edge = call(
+        edge_kernel,
+        (xt, first_edges, second_edges, first_got, second_got),
+        [
+            pltpu.VMEM((rows + 1,) + plane, bf16),
+            pltpu.VMEM((layers + 1,) + plane, bf16),
+            pltpu.VMEM(plane, bf16),
+            pltpu.VMEM((layers,) + plane, f32),
+        ],
+    )
+    packet = in_vmem(lax.ppermute(packet, "section", ahead))
+    work = [
+        pltpu.VMEM((3, rows + 2, 2 * channels, LANES), bf16),
+        pltpu.VMEM((rows, gate_count, LANES), bf16),
+        pltpu.VMEM((gate_count * rows, LANES), bf16),
+        pltpu.SemaphoreType.DMA((gate_count * rows // 512,)),
+    ]
+    gates_shape = jax.ShapeDtypeStruct((steps, layers, gate_count * rows, LANES), bf16)
+    fresh = [pltpu.VMEM((rows + 1,) + plane, bf16), pltpu.VMEM((flat, LANES), f32), gates_shape]
+    last, last_memory, gates = call(
+        first_last_layer,
+        (xt, packed, weights, wide_bias, cells, cell_edge),
+        fresh,
+        work,
+        places=([VMEM] * 6, [VMEM, VMEM, ANY]),
+    )
+    next_packet = in_vmem(lax.ppermute(last, "section", ahead))
+    before, before_memory, gates = call(
+        first_first_layer,
+        (xt, packet, packed, weights, wide_bias, cells, cell_edge, gates),
+        fresh,
+        work,
+        aliases={7: 2},
+        places=([VMEM] * 7 + [ANY], [VMEM, VMEM, ANY]),
+    )
+    final = [
+        gates_shape,
+        jax.ShapeDtypeStruct((layers, flat, LANES), bf16),
+        jax.ShapeDtypeStruct((layers, flat, LANES), f32),
+    ]
+    close = work + [
+        pltpu.VMEM((rows,) + plane, bf16),
+        pltpu.VMEM((flat, LANES), bf16),
+        pltpu.VMEM((flat, LANES), f32),
+        pltpu.SemaphoreType.DMA((2,)),
+    ]
+    gates, hidden_out, memory_out = call(
+        second_last_layer,
+        (before, last, weights, wide_bias, last_memory, gates),
+        final,
+        close,
+        aliases={5: 0},
+        places=([VMEM] * 5 + [ANY], [ANY] * 3),
+    )
+    gates, hidden_out, memory_out = call(
+        second_first_layer,
+        (xt, next_packet, next_edge, before, weights, wide_bias, before_memory, gates, hidden_out, memory_out),
+        final,
+        close,
+        aliases={7: 0, 8: 1, 9: 2},
+        places=([VMEM] * 7 + [ANY] * 3, [ANY] * 3),
+    )
+    return (
+        hidden_out.reshape(layers, 1, channels, rows, LANES),
+        memory_out.reshape(layers, 1, channels, rows, LANES),
+        gates.reshape(steps, layers, 1, gate_count, rows, LANES),
+    )
 
 
 def from_behind(block, axis, distance):
@@ -18,17 +491,13 @@
     return lax.ppermute(shard, axis, pairs)
 
 
-def tile_place():
-    place = (lax.axis_index("tile") + GRID_COLS + GRID_COLS // 2) % lax.axis_size("tile")
-    return (place // GRID_COLS, place % GRID_COLS)
-
-
 def keep_if(condition, rim):
     return jnp.where(condition, rim, jnp.zeros_like(rim))
 
 
 def with_rims(source_field):
-    row_place, column_place = tile_place()
+    place = tile_place()
+    row_place, column_place = (place // GRID_COLS, place % GRID_COLS)
     grid_rows = lax.axis_size("tile") // GRID_COLS
     upper_rim = from_behind(source_field[:, -1:, :], "tile", GRID_COLS)
     lower_rim = from_behind(source_field[:, :1, :], "tile", -GRID_COLS)
@@ -72,7 +541,7 @@
     return (hidden_state, memory, opened)
 
 
-def body(frames, hidden_init, memory_init, weights, biases):
+def general_body(frames, hidden_init, memory_init, weights, biases):
     step_count = frames.shape[0]
     layer_count = weights.shape[0]
     channels = frames.shape[2]
@@ -110,6 +579,13 @@
     return (hidden_out, memory_out, gates_out)
 
 
+def body(frames, hidden_init, memory_init, weights, biases):
+    one_row = lax.axis_size("tile") == GRID_COLS
+    if one_row and frames.shape[0] == 2 and weights.shape[0] == 2:
+        return wavefront(frames, hidden_init, memory_init, weights, biases)
+    return general_body(frames, hidden_init, memory_init, weights, biases)
+
+
 def solution(mesh):
     in_specs = (
         P(None, ("member", "tile"), None, None, None),

time: 87.6 us -> 44.8 us (0.51)
  other arithmetic: 24.9 us -> 0.01 us
  Pallas kernels: 0 us -> 20.7 us
  local copies, waits for them, and re-layouts: 20.1 us -> 6.33 us
  matrix products: 10.5 us -> 0 us
  waiting for transfers between devices: 13.3 us -> 3.04 us
  starting transfers between devices: 16.9 us -> 13.4 us
    pallas_call x0 -> x6, Pallas kernels: none -> 20.7 us  [call(): pl.pallas_call(kernel, in_specs=places[0] if places else [VMEM] * len(ins...]
    another operation x16 -> x0, other arithmetic: 13.5 us -> none
    dot_general x4 -> x0, matrix products: 10.5 us -> none  [advance(): jnp.dot(layer_weights, patches, preferred_element_type=jnp.float32)]
    ppermute x10 -> x4, waiting for transfers between devices: 13.3 us -> 3.04 us  [the longest x1 3.03 us: wavefront(): second_got = in_vmem(lax.ppermute(second_edges, 'tile', swap_pairs(1)))]
    another operation x4 -> x0, local copies, waits for them, and re-layouts: 5.82 us -> none  [advance(): jnp.stack([inflow, forget, outflow, candidate])]
    slice x10 -> x0, local copies, waits for them, and re-layouts: 4.55 us -> none  [the longest x1 1.27 us: body(): memory_init[layer_index, 0]]
    ppermute x10 -> x4, starting transfers between devices: 16.9 us -> 13.4 us  [the longest x1 5.44 us: wavefront(): second_got = in_vmem(lax.ppermute(second_edges, 'tile', swap_pairs(1)))]
    convert_element_type x4 -> x0, other arithmetic: 3.51 us -> none  [advance(): hidden_state = (outflow * jnp.tanh(memory)).astype(jnp.bfloat16)]
  transfers between devices with their start and end apart: 10 -> 4, of which waited for: 5 -> 1; matrix products, arithmetic and copies ran while one was open for 12% -> 0% of each run, Pallas kernels for 0% -> 31%
where the time goes in v1:
time: 44.8 us; the launch traced here: 44.4 us
  Pallas kernels  20.7 us (46%)
  starting transfers between devices  13.4 us (30%)
  local copies, waits for them, and re-layouts  6.33 us (14%)
  waiting for transfers between devices  3.04 us (7%)
  between operations  0.93 us (2%)
    pallas_call x6, Pallas kernels, call(): pl.pallas_call(kernel, in_specs=places[0] if places else [VMEM] * len(ins...  20.7 us
    unnamed x14, local copies, waits for them, and re-layouts  6.33 us
    ppermute x1, starting transfers between devices, wavefront(): second_got = in_vmem(lax.ppermute(second_edges, 'tile', swap_pairs(1)))  5.44 us
    ppermute x1, starting transfers between devices, wavefront(): packet = in_vmem(lax.ppermute(packet, 'section', ahead))  3.41 us
    ppermute x1, starting transfers between devices, wavefront(): first_got = in_vmem(lax.ppermute(first_edges, 'tile', swap_pairs(0)))  3.06 us
    ppermute x1, waiting for transfers between devices, wavefront(): second_got = in_vmem(lax.ppermute(second_edges, 'tile', swap_pairs(1)))  3.03 us
    ppermute x1, starting transfers between devices, wavefront(): next_packet = in_vmem(lax.ppermute(last, 'section', ahead))  1.49 us
  transfers between devices with their start and end apart: 4, of which 1 were waited for; matrix products, arithmetic and copies ran while one was open for 0% of the time, Pallas kernels for 31%

profile of v1, /device:TPU:0, one launch (start us, length us, event | category | flops | bytes accessed | tf_op | source)
XLA Modules:
  0.0 44.4 jit_solution(3737564590248159367)
XLA Ops:
  0.6 0.0 copy-start.1
  0.6 1.2 %copy-done.1 = f32[2,1,128,8,128]{4,3,2,1,0:T(8,128)S(1)} copy-done((f32[2,1,128,8,128]{4,3,2,1,0:T(8,128)S(1)}, f32[2,1,128,8,128]{4,3,2,1,0:T(8,128)}, u32[]{:S(2)}) %copy-start.1) | copy-done | bytes 1048600
  1.9 0.0 copy-start.2
  1.9 1.0 %copy-done.2 = bf16[2,1,128,8,128]{4,3,2,1,0:T(8,128)(2,1)S(1)} copy-done((bf16[2,1,128,8,128]{4,3,2,1,0:T(8,128)(2,1)S(1)}, bf16[2,1,128,8,128]{4,3,2,1,0:T(8,128)(2,1)}, u32[]{:S(2)}) %copy-start.2) | copy-done | bytes 524312
  2.9 0.0 copy-start.3
  2.9 1.0 %copy-done.3 = bf16[2,1,128,8,128]{4,3,2,1,0:T(8,128)(2,1)S(1)} copy-done((bf16[2,1,128,8,128]{4,3,2,1,0:T(8,128)(2,1)S(1)}, bf16[2,1,128,8,128]{4,3,2,1,0:T(8,128)(2,1)}, u32[]{:S(2)}) %copy-start.3) | copy-done | bytes 524312
  3.9 0.0 copy-start.4
  3.9 0.7 %copy-done.4 = f32[2,512]{1,0:T(2,128)S(1)} copy-done((f32[2,512]{1,0:T(2,128)S(1)}, f32[2,512]{1,0:T(2,128)}, u32[]{:S(2)}) %copy-start.4) | copy-done | bytes 4120
  4.6 2.0 %shard_map.76 = (bf16[8,512,128]{2,1,0:T(8,128)(2,1)S(1)}, bf16[128,128]{1,0:T(8,128)(2,1)S(1)}, bf16[128,128]{1,0:T(8,128)(2,1)S(1)}, f32[2,1024,128]{2,1,0:T(8,128)S(1)}, f32[2,512,128]{2,1,0:T(8,128)S(1)}) custom-call(bf16[2,1024,128]{2,1,0:T(8,128)(2,1)S(1)} %bitcast.15, bf16[2,1024,128]{2,1,0:T(8,128)(2,1)S(1)} %bitcast.16, ...), custom_call_target="tpu_custom_call" | custom-call | tf_op jit(solution)/shard_map/pallas_call | solution.py:388
  6.7 3.1 %collective-permute-start = (bf16[128,128]{1,0:T(8,128)(2,1)S(1)}, bf16[128,128]{1,0:T(8,128)(2,1)S(1)}, u32[]{:S(2)}, u32[]{:S(2)}) collective-permute-start(bf16[128,128]{1,0:T(8,128)(2,1)S(1)} %get-tuple-element.25.first_own), channel_id=1, source_target_pairs={{8,10},{10,8},{12,14},{14,12},{0,2},{2,0},{4,6},{6,4},{9,11},{11,9... | collective-permute-start | bytes 98312 | tf_op jit(solution)/shard_map/ppermute | solution.py:411
  9.7 5.4 %collective-permute-start.1 = (bf16[128,128]{1,0:T(8,128)(2,1)S(1)}, bf16[128,128]{1,0:T(8,128)(2,1)S(1)}, u32[]{:S(2)}, u32[]{:S(2)}) collective-permute-start(bf16[128,128]{1,0:T(8,128)(2,1)S(1)} %get-tuple-element.26.second_own), channel_id=1, source_target_pairs={{10,12},{12,10},{14,0},{0,14},{2,4},{4,2},{11,13},{13,11},{15,1},{... | collective-permute-start | bytes 98312 | tf_op jit(solution)/shard_map/ppermute | solution.py:412
  15.2 0.0 collective-permute-done.first_got
  15.2 3.0 %collective-permute-done.1.second_got = bf16[128,128]{1,0:T(8,128)(2,1)S(1)} collective-permute-done((bf16[128,128]{1,0:T(8,128)(2,1)S(1)}, bf16[128,128]{1,0:T(8,128)(2,1)S(1)}, u32[]{:S(2)}, u32[]{:S(2)}) %collective-permute-start.1) | collective-permute-done | bytes 32800 | tf_op jit(solution)/shard_map/ppermute | solution.py:412
  18.2 0.5 %shard_map.77 = (bf16[9,128,128]{2,1,0:T(8,128)(2,1)S(1)}, bf16[3,128,128]{2,1,0:T(8,128)(2,1)S(1)}, bf16[128,128]{1,0:T(8,128)(2,1)S(1)}, f32[2,128,128]{2,1,0:T(8,128)S(1)}) custom-call(bf16[8,512,128]{2,1,0:T(8,128)(2,1)S(1)} %get-tuple-element.24.xt, bf16[128,128]{1,0:T(8,128)(2,1)S(1)} %get-tuple-element.25.first_own, ...), custom_call_target="tpu_custom_call" | custom-call | tf_op jit(solution)/shard_map/pallas_call | solution.py:388
  18.8 3.4 %collective-permute-start.3 = (bf16[9,128,128]{2,1,0:T(8,128)(2,1)S(1)}, bf16[9,128,128]{2,1,0:T(8,128)(2,1)S(1)}, u32[]{:S(2)}, u32[]{:S(2)}) collective-permute-start(bf16[9,128,128]{2,1,0:T(8,128)(2,1)S(1)} %get-tuple-element.33), channel_id=1, source_target_pairs={{0,16},{1,17},{2,18},{3,19},{4,20},{5,21},{6,22},{7,23},{8,24},{9,... | collective-permute-start | bytes 884744 | tf_op jit(solution)/shard_map/ppermute | solution.py:423
  22.2 0.0 copy-start
  22.2 2.3 %copy-done = bf16[2,512,2304]{2,1,0:T(8,128)(2,1)S(1)} copy-done((bf16[2,512,2304]{2,1,0:T(8,128)(2,1)S(1)}, bf16[2,512,2304]{2,1,0:T(8,128)(2,1)}, u32[]{:S(2)}) %copy-start) | copy-done | bytes 4718616
  24.5 0.0 slice-start
  24.5 4.6 %shard_map.78 = (bf16[9,128,128]{2,1,0:T(8,128)(2,1)S(1)}, f32[1024,128]{1,0:T(8,128)S(1)}, bf16[2,2,4096,128]{3,2,1,0:T(8,128)(2,1)}) custom-call(bf16[8,512,128]{2,1,0:T(8,128)(2,1)S(1)} %get-tuple-element.24.xt, bf16[3,128,128]{2,1,0:T(8,128)(2,1)S(1)} %get-tuple-element.27.packed, bf16[2,512,2304]{2,1,0:T(8,128)(2,1)S(1)} %copy-done, ...), custom_call_target="tpu_custom_call" | custom-call | tf_op jit(solution)/shard_map/pallas_call | solution.py:388
  29.1 1.5 %collective-permute-start.2 = (bf16[9,128,128]{2,1,0:T(8,128)(2,1)S(1)}, bf16[9,128,128]{2,1,0:T(8,128)(2,1)S(1)}, u32[]{:S(2)}, u32[]{:S(2)}) collective-permute-start(bf16[9,128,128]{2,1,0:T(8,128)(2,1)S(1)} %get-tuple-element.31.last), channel_id=1, source_target_pairs={{0,16},{1,17},{2,18},{3,19},{4,20},{5,21},{6,22},{7,23},{8,24},{9,... | collective-permute-start | bytes 884744 | tf_op jit(solution)/shard_map/ppermute | solution.py:439
  30.6 0.0 collective-permute-done.3.packet
  30.6 0.0 slice-start.1
  30.6 4.6 %shard_map.79 = (bf16[9,128,128]{2,1,0:T(8,128)(2,1)S(1)}, f32[1024,128]{1,0:T(8,128)S(1)}, bf16[2,2,4096,128]{3,2,1,0:T(8,128)(2,1)}) custom-call(bf16[8,512,128]{2,1,0:T(8,128)(2,1)S(1)} %get-tuple-element.24.xt, bf16[9,128,128]{2,1,0:T(8,128)(2,1)S(1)} %collective-permute-done.3.packet, ...), custom_call_target="tpu_custom_call", output_to_operand_aliasing={{2}: (7, {})} | custom-call | tf_op jit(solution)/shard_map/pallas_call | solution.py:388
  35.2 0.0 slice-done
  35.2 0.0 slice-done.1
  35.2 4.5 %shard_map.80 = (bf16[2,2,4096,128]{3,2,1,0:T(8,128)(2,1)}, bf16[2,1024,128]{2,1,0:T(8,128)(2,1)}, f32[2,1024,128]{2,1,0:T(8,128)}) custom-call(bf16[9,128,128]{2,1,0:T(8,128)(2,1)S(1)} %get-tuple-element.35.before.last, bf16[9,128,128]{2,1,0:T(8,128)(2,1)S(1)} %get-tuple-element.31.last, ...), custom_call_target="tpu_custom_call", output_to_operand_aliasing={{0}: (5, {})} | custom-call | tf_op jit(solution)/shard_map/pallas_call | solution.py:388
  39.8 0.0 collective-permute-done.2.packet
  39.8 4.5 %shard_map.81 = (bf16[2,2,4096,128]{3,2,1,0:T(8,128)(2,1)}, bf16[2,1024,128]{2,1,0:T(8,128)(2,1)}, f32[2,1024,128]{2,1,0:T(8,128)}) custom-call(bf16[8,512,128]{2,1,0:T(8,128)(2,1)S(1)} %get-tuple-element.24.xt, bf16[9,128,128]{2,1,0:T(8,128)(2,1)S(1)} %collective-permute-done.2.packet, ...), custom_call_target="tpu_custom_call", output_to_operand_aliasing={{0}: (7, {}), {1}: (8, {}), {2}: (9, {})} | custom-call | tf_op jit(solution)/shard_map/pallas_call | solution.py:388
  (1 shorter events, 0.0 us)
Async XLA Ops:
  0.6 1.2 %copy-start.1 = (f32[2,1,128,8,128]{4,3,2,1,0:T(8,128)S(1)}, f32[2,1,128,8,128]{4,3,2,1,0:T(8,128)}, u32[]{:S(2)}) copy-start(f32[2,1,128,8,128]{4,3,2,1,0:T(8,128)} %param.7) | copy-start | bytes 3145732
  1.9 1.0 %copy-start.2 = (bf16[2,1,128,8,128]{4,3,2,1,0:T(8,128)(2,1)S(1)}, bf16[2,1,128,8,128]{4,3,2,1,0:T(8,128)(2,1)}, u32[]{:S(2)}) copy-start(bf16[2,1,128,8,128]{4,3,2,1,0:T(8,128)(2,1)} %param.5) | copy-start | bytes 1572868
  2.9 1.0 %copy-start.3 = (bf16[2,1,128,8,128]{4,3,2,1,0:T(8,128)(2,1)S(1)}, bf16[2,1,128,8,128]{4,3,2,1,0:T(8,128)(2,1)}, u32[]{:S(2)}) copy-start(bf16[2,1,128,8,128]{4,3,2,1,0:T(8,128)(2,1)} %param.6) | copy-start | bytes 1572868
  3.9 0.7 %copy-start.4 = (f32[2,512]{1,0:T(2,128)S(1)}, f32[2,512]{1,0:T(2,128)}, u32[]{:S(2)}) copy-start(f32[2,512]{1,0:T(2,128)} %bias.1) | copy-start | bytes 12292
  6.7 8.5 %collective-permute-start = (bf16[128,128]{1,0:T(8,128)(2,1)S(1)}, bf16[128,128]{1,0:T(8,128)(2,1)S(1)}, u32[]{:S(2)}, u32[]{:S(2)}) collective-permute-start(bf16[128,128]{1,0:T(8,128)(2,1)S(1)} %get-tuple-element.25.first_own), channel_id=1, source_target_pairs={{8,10},{10,8},{12,14},{14,12},{0,2},{2,0},{4,6},{6,4},{9,11},{11,9... | collective-permute-start | bytes 98312 | tf_op jit(solution)/shard_map/ppermute | solution.py:411
  9.7 8.5 %collective-permute-start.1 = (bf16[128,128]{1,0:T(8,128)(2,1)S(1)}, bf16[128,128]{1,0:T(8,128)(2,1)S(1)}, u32[]{:S(2)}, u32[]{:S(2)}) collective-permute-start(bf16[128,128]{1,0:T(8,128)(2,1)S(1)} %get-tuple-element.26.second_own), channel_id=1, source_target_pairs={{10,12},{12,10},{14,0},{0,14},{2,4},{4,2},{11,13},{13,11},{15,1},{... | collective-permute-start | bytes 98312 | tf_op jit(solution)/shard_map/ppermute | solution.py:412
  18.8 11.8 %collective-permute-start.3 = (bf16[9,128,128]{2,1,0:T(8,128)(2,1)S(1)}, bf16[9,128,128]{2,1,0:T(8,128)(2,1)S(1)}, u32[]{:S(2)}, u32[]{:S(2)}) collective-permute-start(bf16[9,128,128]{2,1,0:T(8,128)(2,1)S(1)} %get-tuple-element.33), channel_id=1, source_target_pairs={{0,16},{1,17},{2,18},{3,19},{4,20},{5,21},{6,22},{7,23},{8,24},{9,... | collective-permute-start | bytes 884744 | tf_op jit(solution)/shard_map/ppermute | solution.py:423
  22.2 2.3 %copy-start = (bf16[2,512,2304]{2,1,0:T(8,128)(2,1)S(1)}, bf16[2,512,2304]{2,1,0:T(8,128)(2,1)}, u32[]{:S(2)}) copy-start(bf16[2,512,2304]{2,1,0:T(8,128)(2,1)} %weights.7) | copy-start | bytes 14155780
  24.5 10.7 %slice-start = ((s8[4718592]{0:T(1024)(128)(4,1)}), s8[4194304]{0:T(1024)(128)(4,1)S(1)}, s32[]{:S(2)}) async-start(s8[4718592]{0:T(1024)(128)(4,1)} %bitcast.12), calls=%async_computation | async-start | bytes 8388608
  29.1 10.7 %collective-permute-start.2 = (bf16[9,128,128]{2,1,0:T(8,128)(2,1)S(1)}, bf16[9,128,128]{2,1,0:T(8,128)(2,1)S(1)}, u32[]{:S(2)}, u32[]{:S(2)}) collective-permute-start(bf16[9,128,128]{2,1,0:T(8,128)(2,1)S(1)} %get-tuple-element.31.last), channel_id=1, source_target_pairs={{0,16},{1,17},{2,18},{3,19},{4,20},{5,21},{6,22},{7,23},{8,24},{9,... | collective-permute-start | bytes 884744 | tf_op jit(solution)/shard_map/ppermute | solution.py:439
  30.6 4.6 %slice-start.1 = ((s8[4718592]{0:T(1024)(128)(4,1)}), s8[524288]{0:T(1024)(128)(4,1)S(1)}, s32[]{:S(2)}) async-start(s8[4718592]{0:T(1024)(128)(4,1)} %bitcast.12), calls=%async_computation.1 | async-start | bytes 1048576

commit v2 on v0

--- a/solution.py
+++ b/solution.py
@@ -1,9 +1,551 @@
+import functools
+
 import jax
 import jax.numpy as jnp
 from jax import lax
+from jax.experimental import pallas as pl
+from jax.experimental.pallas import tpu as pltpu
 from jax.sharding import PartitionSpec as P
 
+
 GRID_COLS = 8
+LANES = 128
+
+bf16 = jnp.bfloat16
+f32 = jnp.float32
+VMEM = pl.BlockSpec(memory_space=pltpu.VMEM)
+HBM = pl.BlockSpec(memory_space=pltpu.HBM)
+
+
+def iota(shape, dim):
+    return lax.broadcasted_iota(jnp.int32, shape, dim)
+
+
+def params():
+    return pltpu.CompilerParams(vmem_limit_bytes=24 * 2**20)
+
+
+def in_vmem(array):
+    return pltpu.with_memory_space_constraint(array, pltpu.VMEM)
+
+
+def in_hbm(array):
+    return pltpu.with_memory_space_constraint(array, pltpu.HBM)
+
+
+def permuted(array, axis, pairs):
+    return in_vmem(lax.ppermute(array, axis, pairs))
+
+
+def tile_place():
+    return (lax.axis_index("tile") + GRID_COLS + GRID_COLS // 2) % lax.axis_size("tile")
+
+
+def swap_pairs(parity):
+    count = lax.axis_size("tile")
+    index = {(k + GRID_COLS + GRID_COLS // 2) % count: k for k in range(count)}
+    pairs = []
+    for place in range(count - 1):
+        if place % 2 == parity and place % GRID_COLS != GRID_COLS - 1:
+            pairs += [(index[place], index[place + 1]), (index[place + 1], index[place])]
+    return pairs
+
+
+def swap_matrix(rows, block, to_rows_first):
+    size = rows * block
+    m = iota((size, size), 0)
+    n = iota((size, size), 1)
+    if to_rows_first:
+        m, n = n, m
+    return jnp.where((m // rows == n % block) & (m % rows == n // block), 1.0, 0.0).astype(bf16)
+
+
+def turned(value, by):
+    return pltpu.roll(value, by % LANES, 1)
+
+
+def prep_kernel(
+    frames, hidden, memory, bias, weights, xt, sent, first_edges, second_edges, cells, wide_bias, last_weights,
+    raw, raw_bias, sems,
+):
+    layers, _, _ = hidden.shape
+    rows, channels, _ = sent.shape
+    copies = [
+        pltpu.make_async_copy(hidden, raw.at[pl.ds(0, layers)], sems.at[0]),
+        pltpu.make_async_copy(frames, raw.at[pl.ds(layers, frames.shape[0])], sems.at[1]),
+        pltpu.make_async_copy(memory, cells, sems.at[2]),
+        pltpu.make_async_copy(bias, raw_bias, sems.at[3]),
+        pltpu.make_async_copy(weights.at[layers - 1], last_weights, sems.at[4]),
+    ]
+    for copy in copies:
+        copy.start()
+    block = 256 // rows
+    order = swap_matrix(rows, block, True)
+    count = raw.shape[0]
+    width = rows * LANES
+    m = iota((width, LANES), 0)
+    lane = iota((width, LANES), 1)
+    near = lane // rows
+    to_right = (lane < 2 * rows) & (m == (lane % rows) * LANES + (LANES - 2) + near)
+    to_left = (lane < 2 * rows) & (m == (lane % rows) * LANES + 1 - near)
+    select = jnp.concatenate(
+        [jnp.where(to_right, 1.0, 0.0).astype(bf16), jnp.where(to_left, 1.0, 0.0).astype(bf16)], axis=1
+    )
+    for pair in range(0, count, 2):
+        copies[pair // layers].wait()
+        for group in range(channels // block):
+            part = pl.ds(group * 256, 256)
+            both = jnp.concatenate([raw[pair, part], raw[pair + 1, part]], axis=1)
+            out = jnp.dot(order, both, preferred_element_type=f32).astype(bf16)
+            for r in range(rows):
+                for k in range(2):
+                    piece = out[r * block : (r + 1) * block, k * LANES : (k + 1) * LANES]
+                    at = (pair + k) * channels + group * block
+                    xt[r, at : at + block] = piece
+                    if pair + k == layers - 1:
+                        sent[r, group * block : (group + 1) * block] = piece
+    edge = 2 * rows
+    lane = iota((channels, LANES), 1)
+    cell_right = jnp.zeros((channels, LANES), f32)
+    cell_left = jnp.zeros((channels, LANES), f32)
+    copies[2].wait()
+    for layer in range(layers):
+        for r in range(rows):
+            row = cells[layer, pl.ds(r, channels, stride=rows), :]
+            to = (count + layer) * edge + r
+            cell_right = jnp.where(lane == to, turned(row, to + 1), cell_right)
+            cell_left = jnp.where(lane == to, turned(row, to), cell_left)
+    wide = jnp.concatenate([xt[r] for r in range(rows)], axis=1)
+    edges = jnp.dot(wide, select, preferred_element_type=f32)
+
+    def split(value):
+        high = value.astype(bf16)
+        low = (value - high.astype(f32)).astype(bf16)
+        return high.astype(f32) + turned(low.astype(f32), rows)
+
+    right, left = split(cell_right), split(cell_left)
+    for k in range(count):
+        part = edges[k * channels : (k + 1) * channels]
+        right += turned(part[:, :LANES], k * edge)
+        left += turned(part[:, LANES:], k * edge)
+    even = tile_place() % 2 == 0
+    first_edges[...] = jnp.where(even, right, left).astype(bf16)
+    second_edges[...] = jnp.where(even, left, right).astype(bf16)
+    copies[3].wait()
+    for layer in range(layers):
+        for q in range(4):
+            part = raw_bias[layer : layer + 1, q * channels : (q + 1) * channels]
+            part = jnp.broadcast_to(part, (channels, channels)).T
+            wide_bias[layer, q * channels : (q + 1) * channels] = part * (0.5 if q < 3 else 1.0)
+    copies[4].wait()
+
+
+def cell_step(pre, bias, memory):
+    channels = memory.shape[0]
+
+    def gate(q):
+        part = slice(q * channels, (q + 1) * channels)
+        if q == 3:
+            return jnp.tanh(pre[part] + bias[part])
+        return jnp.tanh(pre[part] * 0.5 + bias[part]) * 0.5 + 0.5
+
+    inflow, forget, outflow, candidate = gate(0), gate(1), gate(2), gate(3)
+    memory = forget * memory + inflow * candidate
+    hidden = (outflow * jnp.tanh(memory)).astype(bf16)
+    return (inflow, forget, outflow, candidate), memory, hidden
+
+
+def run_layer(sources, edge_columns, weights, bias, memory_of, memory_out, hidden_rows, gate_rows, shifted, beside=()):
+    rows = shifted.shape[1] - 2
+    channels = shifted.shape[2] // 2
+    lane = iota((channels, LANES), 1)
+    blank = jnp.zeros((2 * channels, LANES), bf16)
+    for b in range(3):
+        shifted[b, 0] = blank
+        shifted[b, rows + 1] = blank
+
+    def build(r):
+        for k in range(2):
+            part = slice(k * channels, (k + 1) * channels)
+            x = sources[k](r)
+            if edge_columns is None:
+                before = after = jnp.zeros_like(x)
+            else:
+                before = turned(edge_columns[k], -2 * rows - r)
+                after = turned(edge_columns[k], -1 - 3 * rows - r)
+            shifted[1, r + 1, part] = x
+            shifted[0, r + 1, part] = jnp.where(lane == 0, before, turned(x, 1))
+            shifted[2, r + 1, part] = jnp.where(lane == LANES - 1, after, turned(x, -1))
+
+    beside = list(beside)
+    tiles = rows // 2
+    share = -(-len(beside) // tiles)
+    for r in range(min(3, rows)):
+        build(r)
+    for j in range(tiles):
+        patches = jnp.concatenate(
+            [
+                jnp.concatenate([shifted[b, 2 * j + a], shifted[b, 2 * j + a + 1]], axis=1)
+                for a in range(3)
+                for b in range(3)
+            ],
+            axis=0,
+        )
+        total = jnp.dot(weights, patches, preferred_element_type=f32)
+        for r in (2 * j + 3, 2 * j + 4):
+            if r < rows:
+                build(r)
+        for work in beside[j * share : (j + 1) * share]:
+            work()
+        for k in range(2):
+            r = 2 * j + k
+            at = pl.ds(r, channels, stride=rows)
+            gates, memory, hidden = cell_step(total[:, k * LANES : (k + 1) * LANES], bias, memory_of(at))
+            memory_out[at, :] = memory
+            hidden_rows[r] = hidden
+            for q in range(4):
+                gate_rows[r, q * channels : (q + 1) * channels] = gates[q].astype(bf16)
+
+
+def edge_step(columns, weights, bias, memory, rows):
+    channels = memory.shape[0]
+    lane = iota((2 * channels, LANES), 1)
+    parts = []
+    for a in range(3):
+        row = lane % rows + (a - 1)
+        for b in range(3):
+            moved = turned(columns[b], 1 - a)
+            parts.append(jnp.where((row >= 0) & (row < rows), moved, jnp.zeros_like(moved)))
+    total = jnp.dot(weights, jnp.concatenate(parts, axis=0), preferred_element_type=f32)
+    return cell_step(total, bias, memory)
+
+
+def outer_columns(hidden, rows):
+    lane = iota(hidden.shape, 1)
+    place = tile_place() % GRID_COLS
+    inside = ((lane < rows) & (place > 0)) | ((lane >= rows) & (lane < 2 * rows) & (place < GRID_COLS - 1))
+    return turned(jnp.where(inside, hidden, jnp.zeros_like(hidden)), 2 * rows)
+
+
+def restore(source, target, first):
+    rows = source.shape[0]
+    block = 256 // rows
+    order = swap_matrix(rows, block, False)
+    both = []
+    for at in (first // rows, first // rows + block):
+        both.append(jnp.concatenate([source[r, at : at + block] for r in range(rows)], axis=0))
+    out = jnp.dot(order, jnp.concatenate(both, axis=1), preferred_element_type=f32).astype(bf16)
+    target[first : first + 256] = out[:, :LANES]
+    target[first + 256 : first + 512] = out[:, LANES:]
+
+
+def saves(source, tiles, out, sems, started):
+    def piece(first):
+        def work():
+            restore(source, tiles, first)
+            part = pl.ds(first, 512)
+            copy = pltpu.make_async_copy(tiles.at[part], out.at[part], sems.at[first // 512])
+            copy.start()
+            started.append(copy)
+
+        return work
+
+    return [piece(first) for first in range(0, tiles.shape[0], 512)]
+
+
+def part_of(ref, k, channels):
+    def load(r):
+        return ref[r, k * channels : (k + 1) * channels]
+
+    return load
+
+
+def either(condition, one, other):
+    def load(r):
+        return jnp.where(condition, one(r), other(r))
+
+    return load
+
+
+def whole(ref):
+    return lambda r: ref[r]
+
+
+def first_last_layer(xt, last_weights, bias, cells, weights, gate_rows, memory, hidden, first_weights, shifted, sem):
+    layer = bias.shape[0] - 1
+    channels = hidden.shape[1]
+    copy = pltpu.make_async_copy(weights.at[0], first_weights, sem)
+    copy.start()
+    run_layer(
+        (part_of(xt, layer - 1, channels), part_of(xt, layer, channels)),
+        None,
+        last_weights[...],
+        bias[layer],
+        lambda at: cells[layer, at, :],
+        memory,
+        hidden,
+        gate_rows,
+        shifted,
+    )
+    copy.wait()
+
+
+def pack_kernel(rows, first_own, second_own, first_got, second_got, packed, sent, next_edge, taps, cell_edge):
+    channels = sent.shape[0]
+    layers = cell_edge.shape[0]
+    layer = layers - 1
+    edge = 2 * rows
+    even = tile_place() % 2 == 0
+    own_right = jnp.where(even, first_own[...], second_own[...])
+    own_left = jnp.where(even, second_own[...], first_own[...])
+    from_left = jnp.where(even, second_got[...], first_got[...])
+    from_right = jnp.where(even, first_got[...], second_got[...])
+    lane = iota((channels, LANES), 1)
+
+    def laid(k, pieces):
+        out = jnp.zeros((channels, LANES), bf16)
+        for slot, (value, block) in enumerate(pieces):
+            value = turned(value, (slot - block) * rows - k * edge)
+            out = jnp.where((lane >= slot * rows) & (lane < (slot + 1) * rows), value, out)
+        return out
+
+    outer = [(from_left, 0), (own_right, 1), (from_left, 1), (from_right, 1), (own_left, 1), (from_right, 0)]
+    for k in range(layers + 1):
+        packed[k] = laid(k, outer)
+    sent[...] = packed[layer]
+    next_edge[...] = laid(layers + 1, outer)
+    inner = [
+        [(from_left, 0), (own_right, 1), (from_left, 1), (own_right, 0)],
+        [(from_left, 1), (from_right, 1), (own_left, 1), (own_right, 1)],
+        [(own_left, 1), (from_right, 0), (own_left, 0), (from_right, 1)],
+    ]
+    for b in range(3):
+        for k in range(2):
+            taps[b, k * channels : (k + 1) * channels] = laid(layer - 1 + k, inner[b])
+    for k in range(layers):
+        high, low = (
+            laid(layers + 2 + k, [(value, part) for value in (from_left, from_right, own_left, own_right)])
+            for part in range(2)
+        )
+        cell_edge[k] = high.astype(f32) + low.astype(f32)
+
+
+def mend_kernel(taps, last_weights, bias, cell_edge, gate_rows, memory, hidden, last, new_memory, new_gates):
+    rows, channels, _ = hidden.shape
+    layer = bias.shape[0] - 1
+    gates, edge_memory, edge_hidden = edge_step(
+        [taps[b] for b in range(3)], last_weights[...], bias[layer], cell_edge[layer], rows
+    )
+    last[rows] = outer_columns(edge_hidden, rows)
+    gates = jnp.concatenate([gate.astype(bf16) for gate in gates], axis=0)
+
+    def mended(value, column, r):
+        lane = iota(value.shape, 1)
+        value = jnp.where(lane == 0, turned(column, -2 * rows - r), value)
+        return jnp.where(lane == LANES - 1, turned(column, -1 - 3 * rows - r), value)
+
+    for r in range(rows):
+        last[r] = mended(hidden[r], edge_hidden, r)
+    for r in range(rows):
+        at = pl.ds(r, channels, stride=rows)
+        new_memory[at, :] = mended(memory[at, :], edge_memory, r)
+        new_gates[r] = mended(gate_rows[r], gates, r)
+
+
+def middle_kernel(
+    xt, packet, packet_edge, packed, first_weights, last_weights, bias, cells, cell_edge, gate_rows, last, last_memory,
+    before, before_memory, next_gates, next_memory, next_hidden, gates,
+    shifted, first_gates, tiles, other_tiles, sems,
+):
+    first = lax.axis_index("section") == 0
+    rows, channels, _ = packet.shape
+    layers = bias.shape[0]
+    started = []
+    edges = (jnp.where(first, packed[layers], packet_edge[...]), packed[0])
+    run_layer(
+        (either(first, part_of(xt, layers, channels), whole(packet)), part_of(xt, 0, channels)),
+        edges,
+        first_weights[...],
+        bias[0],
+        lambda at: cells[0, at, :],
+        before_memory,
+        before,
+        first_gates,
+        shifted,
+        saves(gate_rows, tiles, gates.at[0, layers - 1], sems.at[0], started),
+    )
+    wide = jnp.concatenate(edges, axis=0)
+    columns = [turned(wide, -2 * rows * b) for b in range(3)]
+    _, _, hidden = edge_step(columns, first_weights[...], bias[0], cell_edge[0], rows)
+    before[rows] = outer_columns(hidden, rows)
+    run_layer(
+        (whole(before), whole(last)),
+        (before[rows], last[rows]),
+        last_weights[...],
+        bias[layers - 1],
+        lambda at: last_memory[at, :],
+        next_memory,
+        next_hidden,
+        next_gates,
+        shifted,
+        saves(first_gates, other_tiles, gates.at[0, 0], sems.at[1], started),
+    )
+    for copy in started:
+        copy.wait()
+
+
+def final_kernel(
+    xt, packet, next_edge, before, first_weights, bias, before_memory, last_gates, last_memory, last_hidden, _,
+    gates, hidden_out, memory_out,
+    shifted, first_gates, tiles, other_tiles, first_hidden, first_memory, hidden_tiles, other_hidden, sems, cell_sems,
+):
+    first = lax.axis_index("section") == 0
+    rows = packet.shape[0] - 1
+    channels = packet.shape[1]
+    layer = bias.shape[0] - 1
+    started = [pltpu.make_async_copy(last_memory, memory_out.at[layer], cell_sems.at[0])]
+    started[0].start()
+    frame = xt.shape[1] // channels - 1
+    run_layer(
+        (either(first, part_of(xt, frame, channels), whole(packet)), whole(before)),
+        (jnp.where(first, next_edge[...], packet[rows]), before[rows]),
+        first_weights[...],
+        bias[0],
+        lambda at: before_memory[at, :],
+        first_memory,
+        first_hidden,
+        first_gates,
+        shifted,
+        saves(last_gates, tiles, gates.at[1, layer], sems.at[0], started)
+        + saves(last_hidden, hidden_tiles, hidden_out.at[layer], sems.at[2], started),
+    )
+    copy = pltpu.make_async_copy(first_memory, memory_out.at[0], cell_sems.at[1])
+    copy.start()
+    started.append(copy)
+    for work in saves(first_gates, other_tiles, gates.at[1, 0], sems.at[1], started):
+        work()
+    for work in saves(first_hidden, other_hidden, hidden_out.at[0], sems.at[3], started):
+        work()
+    for copy in started:
+        copy.wait()
+
+
+def wavefront(frames, hidden_init, memory_init, weights, biases):
+    steps, _, channels, rows, _ = frames.shape
+    layers, gate_count, depth = weights.shape
+    flat = channels * rows
+    frames = in_hbm(frames.reshape(steps, flat, LANES))
+    hidden_init = in_hbm(hidden_init.reshape(layers, flat, LANES))
+    memory_init = in_hbm(memory_init.reshape(layers, flat, LANES))
+    weights, biases = in_hbm(weights), in_hbm(biases)
+    plane = (channels, LANES)
+    sections = lax.axis_size("section")
+    ahead = [(i, i + 1) for i in range(sections - 1)]
+
+    def call(kernel, ins, outs, scratch=(), hbm=(), out_specs=None, aliases=None):
+        return pl.pallas_call(
+            kernel,
+            in_specs=[HBM if i in hbm else VMEM for i in range(len(ins))],
+            out_specs=out_specs or [VMEM] * len(outs),
+            out_shape=outs,
+            scratch_shapes=list(scratch),
+            input_output_aliases=aliases or {},
+            compiler_params=params(),
+        )(*ins)
+
+    state = pltpu.VMEM((rows,) + plane, bf16)
+    state_and_edge = pltpu.VMEM((rows + 1,) + plane, bf16)
+    memory = pltpu.VMEM((flat, LANES), f32)
+    edge = pltpu.VMEM(plane, bf16)
+    layer_weights = pltpu.VMEM((gate_count, depth), bf16)
+    gate_rows = pltpu.VMEM((rows, gate_count, LANES), bf16)
+    shifted = pltpu.VMEM((3, rows + 2, 2 * channels, LANES), bf16)
+    gate_tiles = pltpu.VMEM((gate_count * rows, LANES), bf16)
+    hidden_tiles = pltpu.VMEM((flat, LANES), bf16)
+    pieces = gate_count * rows // 512
+
+    xt, sent, first_edges, second_edges, cells, wide_bias, last_weights = call(
+        prep_kernel,
+        (frames, hidden_init, memory_init, biases, weights),
+        [
+            pltpu.VMEM((rows, (layers + steps) * channels, LANES), bf16),
+            state,
+            edge,
+            edge,
+            pltpu.VMEM((layers, flat, LANES), f32),
+            pltpu.VMEM((layers, gate_count, LANES), f32),
+            layer_weights,
+        ],
+        [
+            pltpu.VMEM((layers + steps, flat, LANES), bf16),
+            pltpu.VMEM((layers, gate_count), f32),
+            pltpu.SemaphoreType.DMA((5,)),
+        ],
+        hbm=range(5),
+    )
+    packet = permuted(sent, "section", ahead)
+    first_got = permuted(first_edges, "tile", swap_pairs(0))
+    second_got = permuted(second_edges, "tile", swap_pairs(1))
+    rough_gates, rough_memory, rough_hidden, first_weights = call(
+        first_last_layer,
+        (xt, last_weights, wide_bias, cells, weights),
+        [gate_rows, memory, state, layer_weights],
+        [shifted, pltpu.SemaphoreType.DMA],
+        hbm=(4,),
+    )
+    packed, sent_edge, next_edge, taps, cell_edge = call(
+        functools.partial(pack_kernel, rows),
+        (first_edges, second_edges, first_got, second_got),
+        [
+            pltpu.VMEM((layers + 1,) + plane, bf16),
+            edge,
+            edge,
+            pltpu.VMEM((3, 2 * channels, LANES), bf16),
+            pltpu.VMEM((layers,) + plane, f32),
+        ],
+    )
+    packet_edge = permuted(sent_edge, "section", ahead)
+    last, last_memory, last_gates = call(
+        mend_kernel,
+        (taps, last_weights, wide_bias, cell_edge, rough_gates, rough_memory, rough_hidden),
+        [state_and_edge, memory, gate_rows],
+    )
+    next_packet = permuted(last, "section", ahead)
+    gates_shape = jax.ShapeDtypeStruct((steps, layers, gate_count * rows, LANES), bf16)
+    before, before_memory, next_gates, next_memory, next_hidden, gates = call(
+        middle_kernel,
+        (
+            xt, packet, packet_edge, packed, first_weights, last_weights, wide_bias, cells, cell_edge,
+            last_gates, last, last_memory,
+        ),
+        [state_and_edge, memory, gate_rows, memory, state, gates_shape],
+        [shifted, gate_rows, gate_tiles, gate_tiles, pltpu.SemaphoreType.DMA((2, pieces))],
+        out_specs=[VMEM] * 5 + [HBM],
+    )
+    gates, hidden_out, memory_out = call(
+        final_kernel,
+        (
+            xt, next_packet, next_edge, before, first_weights, wide_bias, before_memory,
+            next_gates, next_memory, next_hidden, gates,
+        ),
+        [
+            gates_shape,
+            jax.ShapeDtypeStruct((layers, flat, LANES), bf16),
+            jax.ShapeDtypeStruct((layers, flat, LANES), f32),
+        ],
+        [
+            shifted, gate_rows, gate_tiles, gate_tiles, state, memory, hidden_tiles, hidden_tiles,
+            pltpu.SemaphoreType.DMA((4, pieces)), pltpu.SemaphoreType.DMA((2,)),
+        ],
+        hbm=(10,),
+        out_specs=[HBM] * 3,
+        aliases={10: 0},
+    )
+    return (
+        hidden_out.reshape(layers, 1, channels, rows, LANES),
+        memory_out.reshape(layers, 1, channels, rows, LANES),
+        gates.reshape(steps, layers, 1, gate_count, rows, LANES),
+    )
 
 
 def from_behind(block, axis, distance):
@@ -18,17 +560,13 @@
     return lax.ppermute(shard, axis, pairs)
 
 
-def tile_place():
-    place = (lax.axis_index("tile") + GRID_COLS + GRID_COLS // 2) % lax.axis_size("tile")
-    return (place // GRID_COLS, place % GRID_COLS)
-
-
 def keep_if(condition, rim):
     return jnp.where(condition, rim, jnp.zeros_like(rim))
 
 
 def with_rims(source_field):
-    row_place, column_place = tile_place()
+    place = tile_place()
+    row_place, column_place = (place // GRID_COLS, place % GRID_COLS)
     grid_rows = lax.axis_size("tile") // GRID_COLS
     upper_rim = from_behind(source_field[:, -1:, :], "tile", GRID_COLS)
     lower_rim = from_behind(source_field[:, :1, :], "tile", -GRID_COLS)
@@ -72,7 +610,7 @@
     return (hidden_state, memory, opened)
 
 
-def body(frames, hidden_init, memory_init, weights, biases):
+def general_body(frames, hidden_init, memory_init, weights, biases):
     step_count = frames.shape[0]
     layer_count = weights.shape[0]
     channels = frames.shape[2]
@@ -110,6 +648,13 @@
     return (hidden_out, memory_out, gates_out)
 
 
+def body(frames, hidden_init, memory_init, weights, biases):
+    one_row = lax.axis_size("tile") == GRID_COLS
+    if one_row and frames.shape[0] == 2 and weights.shape[0] == 2:
+        return wavefront(frames, hidden_init, memory_init, weights, biases)
+    return general_body(frames, hidden_init, memory_init, weights, biases)
+
+
 def solution(mesh):
     in_specs = (
         P(None, ("member", "tile"), None, None, None),

time: 87.6 us -> 45.9 us (0.52)
  other arithmetic: 24.9 us -> 0 us
  Pallas kernels: 0 us -> 20.9 us
  local copies, waits for them, and re-layouts: 20.1 us -> 0 us
  matrix products: 10.5 us -> 0 us
  waiting for transfers between devices: 13.3 us -> 9.21 us
  starting transfers between devices: 16.9 us -> 14.7 us
    pallas_call x0 -> x6, Pallas kernels: none -> 20.9 us  [call(): pl.pallas_call(kernel, in_specs=[HBM if i in hbm else VMEM for i in range...]
    another operation x16 -> x0, other arithmetic: 13.5 us -> none
    dot_general x4 -> x0, matrix products: 10.5 us -> none  [advance(): jnp.dot(layer_weights, patches, preferred_element_type=jnp.float32)]
    unnamed x67 -> x0, local copies, waits for them, and re-layouts: 9.28 us -> none
    another operation x4 -> x0, local copies, waits for them, and re-layouts: 5.82 us -> none  [advance(): jnp.stack([inflow, forget, outflow, candidate])]
    slice x10 -> x0, local copies, waits for them, and re-layouts: 4.55 us -> none  [the longest x1 1.27 us: body(): memory_init[layer_index, 0]]
    ppermute x10 -> x5, waiting for transfers between devices: 13.3 us -> 9.21 us  [permuted(): return in_vmem(lax.ppermute(array, axis, pairs))]
    convert_element_type x4 -> x0, other arithmetic: 3.51 us -> none  [advance(): hidden_state = (outflow * jnp.tanh(memory)).astype(jnp.bfloat16)]
  transfers between devices with their start and end apart: 10 -> 5, of which waited for: 5 -> 1; matrix products, arithmetic and copies ran while one was open for 12% -> 0% of each run, Pallas kernels for 0% -> 24%
where the time goes in v2:
time: 45.9 us; the launch traced here: 45.7 us
  Pallas kernels  20.9 us (46%)
  starting transfers between devices  14.7 us (32%)
  waiting for transfers between devices  9.21 us (20%)
  between operations  0.88 us (2%)
    pallas_call x6, Pallas kernels, call(): pl.pallas_call(kernel, in_specs=[HBM if i in hbm else VMEM for i in range...  20.9 us
    ppermute x5, starting transfers between devices, permuted(): return in_vmem(lax.ppermute(array, axis, pairs))  14.7 us
    ppermute x5, waiting for transfers between devices, permuted(): return in_vmem(lax.ppermute(array, axis, pairs))  9.21 us
  transfers between devices with their start and end apart: 5, of which 1 were waited for; matrix products, arithmetic and copies ran while one was open for 0% of the time, Pallas kernels for 24%

profile of v2, /device:TPU:0, one launch (start us, length us, event | category | flops | bytes accessed | tf_op | source)
XLA Modules:
  0.0 45.7 jit_solution(13874156365190340935)
XLA Ops:
  0.6 2.8 %shard_map.76 = (bf16[8,512,128]{2,1,0:T(8,128)(2,1)S(1)}, bf16[8,128,128]{2,1,0:T(8,128)(2,1)S(1)}, bf16[128,128]{1,0:T(8,128)(2,1)S(1)}, bf16[128,128]{1,0:T(8...) custom-call(bf16[2,1024,128]{2,1,0:T(8,128)(2,1)} %bitcast.14, ...), custom_call_target="tpu_custom_call" | custom-call | tf_op jit(solution)/shard_map/pallas_call | solution.py:446
  3.4 3.1 %collective-permute-start = (bf16[128,128]{1,0:T(8,128)(2,1)S(1)}, bf16[128,128]{1,0:T(8,128)(2,1)S(1)}, u32[]{:S(2)}, u32[]{:S(2)}) collective-permute-start(bf16[128,128]{1,0:T(8,128)(2,1)S(1)} %get-tuple-element.32.first_own), channel_id=1, source_target_pairs={{8,10},{10,8},{12,14},{14,12},{0,2},{2,0},{4,6},{6,4},{9,11},{11,9... | collective-permute-start | bytes 98312 | tf_op jit(solution)/shard_map/ppermute | solution.py:37
  6.5 5.4 %collective-permute-start.1 = (bf16[128,128]{1,0:T(8,128)(2,1)S(1)}, bf16[128,128]{1,0:T(8,128)(2,1)S(1)}, u32[]{:S(2)}, u32[]{:S(2)}) collective-permute-start(bf16[128,128]{1,0:T(8,128)(2,1)S(1)} %get-tuple-element.33.second_own), channel_id=1, source_target_pairs={{10,12},{12,10},{14,0},{0,14},{2,4},{4,2},{11,13},{13,11},{15,1},{... | collective-permute-start | bytes 98312 | tf_op jit(solution)/shard_map/ppermute | solution.py:37
  11.9 3.0 %shard_map.78 = (bf16[8,512,128]{2,1,0:T(8,128)(2,1)S(1)}, f32[1024,128]{1,0:T(8,128)S(1)}, bf16[8,128,128]{2,1,0:T(8,128)(2,1)S(1)}, bf16[512,2304]{1,0:T(8,128)(2,1)S(1)}) custom-call(bf16[8,512,128]{2,1,0:T(8,128)(2,1)S(1)} %get-tuple-element.31.xt, bf16[512,2304]{1,0:T(8,128)(2,1)S(1)} %get-tuple-element.35.last_weights, ...), custom_call_target="tpu_custom_call" | custom-call | tf_op jit(solution)/shard_map/pallas_call | solution.py:446
  15.0 0.0 collective-permute-done.first_got
  15.0 0.0 collective-permute-done.1.second_got
  15.0 0.4 shard_map.77
  15.4 1.7 %shard_map.79 = (bf16[9,128,128]{2,1,0:T(8,128)(2,1)S(1)}, f32[1024,128]{1,0:T(8,128)S(1)}, bf16[8,512,128]{2,1,0:T(8,128)(2,1)S(1)}) custom-call(bf16[3,256,128]{2,1,0:T(8,128)(2,1)S(1)} %get-tuple-element.34.taps, bf16[512,2304]{1,0:T(8,128)(2,1)S(1)} %get-tuple-element.35.last_weights, f32[2,512,128]{2,1,0:T(8,128)S(1)} %get-tuple-element.36.bias, ...), custom_call_target="tpu_custom_call" | custom-call | tf_op jit(solution)/shard_map/pallas_call | solution.py:446
  17.1 3.4 %collective-permute-start.2 = (bf16[9,128,128]{2,1,0:T(8,128)(2,1)S(1)}, bf16[9,128,128]{2,1,0:T(8,128)(2,1)S(1)}, u32[]{:S(2)}, u32[]{:S(2)}) collective-permute-start(bf16[9,128,128]{2,1,0:T(8,128)(2,1)S(1)} %get-tuple-element.42.last), channel_id=1, source_target_pairs={{0,16},{1,17},{2,18},{3,19},{4,20},{5,21},{6,22},{7,23},{8,24},{9,... | collective-permute-start | bytes 884744 | tf_op jit(solution)/shard_map/ppermute | solution.py:37
  20.5 1.3 %collective-permute-start.3 = (bf16[8,128,128]{2,1,0:T(8,128)(2,1)S(1)}, bf16[8,128,128]{2,1,0:T(8,128)(2,1)S(1)}, u32[]{:S(2)}, u32[]{:S(2)}) collective-permute-start(bf16[8,128,128]{2,1,0:T(8,128)(2,1)S(1)} %get-tuple-element.44), channel_id=1, source_target_pairs={{0,16},{1,17},{2,18},{3,19},{4,20},{5,21},{6,22},{7,23},{8,24},{9,... | collective-permute-start | bytes 786440 | tf_op jit(solution)/shard_map/ppermute | solution.py:37
  21.8 1.5 %collective-permute-start.4 = (bf16[128,128]{1,0:T(8,128)(2,1)S(1)}, bf16[128,128]{1,0:T(8,128)(2,1)S(1)}, u32[]{:S(2)}, u32[]{:S(2)}) collective-permute-start(bf16[128,128]{1,0:T(8,128)(2,1)S(1)} %get-tuple-element.45), channel_id=1, source_target_pairs={{0,16},{1,17},{2,18},{3,19},{4,20},{5,21},{6,22},{7,23},{8,24},{9,... | collective-permute-start | bytes 98312 | tf_op jit(solution)/shard_map/ppermute | solution.py:37
  23.3 9.2 %collective-permute-done.4.packet_edge = bf16[128,128]{1,0:T(8,128)(2,1)S(1)} collective-permute-done((bf16[128,128]{1,0:T(8,128)(2,1)S(1)}, bf16[128,128]{1,0:T(8,128)(2,1)S(1)}, u32[]{:S(2)}, u32[]{:S(2)}) %collective-permute-start.4) | collective-permute-done | bytes 32800 | tf_op jit(solution)/shard_map/ppermute | solution.py:37
  32.5 0.0 collective-permute-done.3.packet
  32.5 8.0 %shard_map.80 = (bf16[9,128,128]{2,1,0:T(8,128)(2,1)S(1)}, f32[1024,128]{1,0:T(8,128)S(1)}, bf16[8,512,128]{2,1,0:T(8,128)(2,1)S(1)}, f32[1024,128]{1,0:T(8,128)...) custom-call(bf16[8,512,128]{2,1,0:T(8,128)(2,1)S(1)} %get-tuple-element.31.xt, ...), custom_call_target="tpu_custom_call" | custom-call | tf_op jit(solution)/shard_map/pallas_call | solution.py:446
  40.5 0.0 collective-permute-done.2.packet
  40.5 5.0 %shard_map.81 = (bf16[2,2,4096,128]{3,2,1,0:T(8,128)(2,1)}, bf16[2,1024,128]{2,1,0:T(8,128)(2,1)}, f32[2,1024,128]{2,1,0:T(8,128)}) custom-call(bf16[8,512,128]{2,1,0:T(8,128)(2,1)S(1)} %get-tuple-element.31.xt, bf16[9,128,128]{2,1,0:T(8,128)(2,1)S(1)} %collective-permute-done.2.packet, ...), custom_call_target="tpu_custom_call", output_to_operand_aliasing={{0}: (10, {})} | custom-call | tf_op jit(solution)/shard_map/pallas_call | solution.py:446
Async XLA Ops:
  3.4 11.5 %collective-permute-start = (bf16[128,128]{1,0:T(8,128)(2,1)S(1)}, bf16[128,128]{1,0:T(8,128)(2,1)S(1)}, u32[]{:S(2)}, u32[]{:S(2)}) collective-permute-start(bf16[128,128]{1,0:T(8,128)(2,1)S(1)} %get-tuple-element.32.first_own), channel_id=1, source_target_pairs={{8,10},{10,8},{12,14},{14,12},{0,2},{2,0},{4,6},{6,4},{9,11},{11,9... | collective-permute-start | bytes 98312 | tf_op jit(solution)/shard_map/ppermute | solution.py:37
  6.5 8.5 %collective-permute-start.1 = (bf16[128,128]{1,0:T(8,128)(2,1)S(1)}, bf16[128,128]{1,0:T(8,128)(2,1)S(1)}, u32[]{:S(2)}, u32[]{:S(2)}) collective-permute-start(bf16[128,128]{1,0:T(8,128)(2,1)S(1)} %get-tuple-element.33.second_own), channel_id=1, source_target_pairs={{10,12},{12,10},{14,0},{0,14},{2,4},{4,2},{11,13},{13,11},{15,1},{... | collective-permute-start | bytes 98312 | tf_op jit(solution)/shard_map/ppermute | solution.py:37
  17.1 23.4 %collective-permute-start.2 = (bf16[9,128,128]{2,1,0:T(8,128)(2,1)S(1)}, bf16[9,128,128]{2,1,0:T(8,128)(2,1)S(1)}, u32[]{:S(2)}, u32[]{:S(2)}) collective-permute-start(bf16[9,128,128]{2,1,0:T(8,128)(2,1)S(1)} %get-tuple-element.42.last), channel_id=1, source_target_pairs={{0,16},{1,17},{2,18},{3,19},{4,20},{5,21},{6,22},{7,23},{8,24},{9,... | collective-permute-start | bytes 884744 | tf_op jit(solution)/shard_map/ppermute | solution.py:37
  20.5 12.0 %collective-permute-start.3 = (bf16[8,128,128]{2,1,0:T(8,128)(2,1)S(1)}, bf16[8,128,128]{2,1,0:T(8,128)(2,1)S(1)}, u32[]{:S(2)}, u32[]{:S(2)}) collective-permute-start(bf16[8,128,128]{2,1,0:T(8,128)(2,1)S(1)} %get-tuple-element.44), channel_id=1, source_target_pairs={{0,16},{1,17},{2,18},{3,19},{4,20},{5,21},{6,22},{7,23},{8,24},{9,... | collective-permute-start | bytes 786440 | tf_op jit(solution)/shard_map/ppermute | solution.py:37
  21.8 10.7 %collective-permute-start.4 = (bf16[128,128]{1,0:T(8,128)(2,1)S(1)}, bf16[128,128]{1,0:T(8,128)(2,1)S(1)}, u32[]{:S(2)}, u32[]{:S(2)}) collective-permute-start(bf16[128,128]{1,0:T(8,128)(2,1)S(1)} %get-tuple-element.45), channel_id=1, source_target_pairs={{0,16},{1,17},{2,18},{3,19},{4,20},{5,21},{6,22},{7,23},{8,24},{9,... | collective-permute-start | bytes 98312 | tf_op jit(solution)/shard_map/ppermute | solution.py:37

commit v3 on v2

--- a/solution.py
+++ b/solution.py
@@ -45,10 +45,14 @@
     count = lax.axis_size("tile")
     index = {(k + GRID_COLS + GRID_COLS // 2) % count: k for k in range(count)}
     pairs = []
-    for place in range(count - 1):
-        if place % 2 == parity and place % GRID_COLS != GRID_COLS - 1:
-            pairs += [(index[place], index[place + 1]), (index[place + 1], index[place])]
+    for place in range(parity, count, 2):
+        one, other = index[place], index[(place + 1) % count]
+        pairs += [(one, other), (other, one)]
     return pairs
+
+
+def halves(value, base):
+    return (value >> (base.bit_length() - 1), value & (base - 1))
 
 
 def swap_matrix(rows, block, to_rows_first):
@@ -57,7 +61,9 @@
     n = iota((size, size), 1)
     if to_rows_first:
         m, n = n, m
-    return jnp.where((m // rows == n % block) & (m % rows == n // block), 1.0, 0.0).astype(bf16)
+    channel, row = halves(m, rows)
+    other_row, other_channel = halves(n, block)
+    return jnp.where((channel == other_channel) & (row == other_row), 1.0, 0.0).astype(bf16)
 
 
 def turned(value, by):
@@ -65,7 +71,7 @@
 
 
 def prep_kernel(
-    frames, hidden, memory, bias, weights, xt, sent, first_edges, second_edges, cells, wide_bias, last_weights,
+    frames, hidden, memory, bias, weights, xt, sent, first_edges, second_edges, cells, wide_bias, half_weights,
     raw, raw_bias, sems,
 ):
     layers, _, _ = hidden.shape
@@ -75,19 +81,31 @@
         pltpu.make_async_copy(frames, raw.at[pl.ds(layers, frames.shape[0])], sems.at[1]),
         pltpu.make_async_copy(memory, cells, sems.at[2]),
         pltpu.make_async_copy(bias, raw_bias, sems.at[3]),
-        pltpu.make_async_copy(weights.at[layers - 1], last_weights, sems.at[4]),
     ]
-    for copy in copies:
+    half = channels // 2
+    for q in range(4):
+        source = weights.at[layers - 1, pl.ds(q * channels, half)]
+        copies.append(pltpu.make_async_copy(source, half_weights.at[pl.ds(q * channels, half)], sems.at[4 + q]))
+    copies[3].start()
+    for copy in copies[:3] + copies[4:]:
         copy.start()
+    copies[3].wait()
+    blocks = [raw_bias[k : k + 1, q * channels : (q + 1) * channels] for k in range(layers) for q in range(4)]
+    columns = jnp.concatenate(blocks + [jnp.zeros((channels - len(blocks), channels), f32)], axis=0).T
+    for k in range(layers):
+        for q in range(4):
+            part = jnp.broadcast_to(columns[:, 4 * k + q : 4 * k + q + 1], (channels, LANES))
+            wide_bias[k, q * channels : (q + 1) * channels] = part * (0.5 if q < 3 else 1.0)
+
     block = 256 // rows
     order = swap_matrix(rows, block, True)
     count = raw.shape[0]
     width = rows * LANES
     m = iota((width, LANES), 0)
     lane = iota((width, LANES), 1)
-    near = lane // rows
-    to_right = (lane < 2 * rows) & (m == (lane % rows) * LANES + (LANES - 2) + near)
-    to_left = (lane < 2 * rows) & (m == (lane % rows) * LANES + 1 - near)
+    near, row = halves(lane, rows)
+    to_right = (lane < 2 * rows) & (m == row * LANES + (LANES - 2) + near)
+    to_left = (lane < 2 * rows) & (m == row * LANES + 1 - near)
     select = jnp.concatenate(
         [jnp.where(to_right, 1.0, 0.0).astype(bf16), jnp.where(to_left, 1.0, 0.0).astype(bf16)], axis=1
     )
@@ -105,25 +123,26 @@
                     if pair + k == layers - 1:
                         sent[r, group * block : (group + 1) * block] = piece
     edge = 2 * rows
-    lane = iota((channels, LANES), 1)
-    cell_right = jnp.zeros((channels, LANES), f32)
-    cell_left = jnp.zeros((channels, LANES), f32)
+    m = iota((2 * LANES, 2 * LANES), 0)
+    part, place = halves(m, LANES)
+    layer_of, place = halves(place, edge)
+    row, side = halves(place, 2)
+    target = side * LANES + (count + layer_of) * edge + part * rows + row
+    spread = (layer_of < layers) & (iota((2 * LANES, 2 * LANES), 1) == target)
+    spread = jnp.where(spread, 1.0, 0.0).astype(bf16)
     copies[2].wait()
+    lane_pair = iota((channels, LANES), 1) >> 1
+    cell_columns = jnp.zeros((channels, LANES), f32)
     for layer in range(layers):
         for r in range(rows):
-            row = cells[layer, pl.ds(r, channels, stride=rows), :]
-            to = (count + layer) * edge + r
-            cell_right = jnp.where(lane == to, turned(row, to + 1), cell_right)
-            cell_left = jnp.where(lane == to, turned(row, to), cell_left)
+            moved = turned(cells[layer, pl.ds(r, channels, stride=rows), :], layer * edge + 2 * r + 1)
+            cell_columns = jnp.where(lane_pair == layer * rows + r, moved, cell_columns)
+    high = cell_columns.astype(bf16)
+    low = (cell_columns - high.astype(f32)).astype(bf16)
     wide = jnp.concatenate([xt[r] for r in range(rows)], axis=1)
     edges = jnp.dot(wide, select, preferred_element_type=f32)
-
-    def split(value):
-        high = value.astype(bf16)
-        low = (value - high.astype(f32)).astype(bf16)
-        return high.astype(f32) + turned(low.astype(f32), rows)
-
-    right, left = split(cell_right), split(cell_left)
+    out = jnp.dot(jnp.concatenate([high, low], axis=1), spread, preferred_element_type=f32)
+    right, left = out[:, :LANES], out[:, LANES:]
     for k in range(count):
         part = edges[k * channels : (k + 1) * channels]
         right += turned(part[:, :LANES], k * edge)
@@ -131,13 +150,8 @@
     even = tile_place() % 2 == 0
     first_edges[...] = jnp.where(even, right, left).astype(bf16)
     second_edges[...] = jnp.where(even, left, right).astype(bf16)
-    copies[3].wait()
-    for layer in range(layers):
-        for q in range(4):
-            part = raw_bias[layer : layer + 1, q * channels : (q + 1) * channels]
-            part = jnp.broadcast_to(part, (channels, channels)).T
-            wide_bias[layer, q * channels : (q + 1) * channels] = part * (0.5 if q < 3 else 1.0)
-    copies[4].wait()
+    for copy in copies[4:]:
+        copy.wait()
 
 
 def cell_step(pre, bias, memory):
@@ -177,42 +191,49 @@
             shifted[0, r + 1, part] = jnp.where(lane == 0, before, turned(x, 1))
             shifted[2, r + 1, part] = jnp.where(lane == LANES - 1, after, turned(x, -1))
 
+    for r in range(rows):
+        build(r)
     beside = list(beside)
     tiles = rows // 2
     share = -(-len(beside) // tiles)
-    for r in range(min(3, rows)):
-        build(r)
-    for j in range(tiles):
-        patches = jnp.concatenate(
-            [
-                jnp.concatenate([shifted[b, 2 * j + a], shifted[b, 2 * j + a + 1]], axis=1)
-                for a in range(3)
-                for b in range(3)
-            ],
-            axis=0,
-        )
-        total = jnp.dot(weights, patches, preferred_element_type=f32)
-        for r in (2 * j + 3, 2 * j + 4):
-            if r < rows:
-                build(r)
-        for work in beside[j * share : (j + 1) * share]:
-            work()
-        for k in range(2):
-            r = 2 * j + k
-            at = pl.ds(r, channels, stride=rows)
-            gates, memory, hidden = cell_step(total[:, k * LANES : (k + 1) * LANES], bias, memory_of(at))
-            memory_out[at, :] = memory
-            hidden_rows[r] = hidden
-            for q in range(4):
-                gate_rows[r, q * channels : (q + 1) * channels] = gates[q].astype(bf16)
+    parts = 1 if beside else 2
+    size = channels // parts
+    for low in range(0, channels, size):
+        chosen = [slice(q * channels + low, q * channels + low + size) for q in range(4)]
+        if parts == 1:
+            part_weights, part_bias = weights, bias
+        else:
+            part_weights = weights(low)
+            part_bias = jnp.concatenate([bias[c] for c in chosen], axis=0)
+        for j in range(tiles):
+            for work in beside[j * share : (j + 1) * share]:
+                work()
+            patches = jnp.concatenate(
+                [
+                    jnp.concatenate([shifted[b, 2 * j + a], shifted[b, 2 * j + a + 1]], axis=1)
+                    for a in range(3)
+                    for b in range(3)
+                ],
+                axis=0,
+            )
+            total = jnp.dot(part_weights, patches, preferred_element_type=f32)
+            for k in range(2):
+                r = 2 * j + k
+                at = pl.ds(r + rows * low, size, stride=rows)
+                gates, memory, hidden = cell_step(total[:, k * LANES : (k + 1) * LANES], part_bias, memory_of(at))
+                memory_out[at, :] = memory
+                hidden_rows[r, low : low + size] = hidden
+                for q in range(4):
+                    gate_rows[r, chosen[q]] = gates[q].astype(bf16)
 
 
 def edge_step(columns, weights, bias, memory, rows):
     channels = memory.shape[0]
     lane = iota((2 * channels, LANES), 1)
     parts = []
+    pixel_row = lane & (rows - 1)
     for a in range(3):
-        row = lane % rows + (a - 1)
+        row = pixel_row + (a - 1)
         for b in range(3):
             moved = turned(columns[b], 1 - a)
             parts.append(jnp.where((row >= 0) & (row < rows), moved, jnp.zeros_like(moved)))
@@ -227,10 +248,9 @@
     return turned(jnp.where(inside, hidden, jnp.zeros_like(hidden)), 2 * rows)
 
 
-def restore(source, target, first):
+def restore(order, source, target, first):
     rows = source.shape[0]
     block = 256 // rows
-    order = swap_matrix(rows, block, False)
     both = []
     for at in (first // rows, first // rows + block):
         both.append(jnp.concatenate([source[r, at : at + block] for r in range(rows)], axis=0))
@@ -239,10 +259,10 @@
     target[first + 256 : first + 512] = out[:, LANES:]
 
 
-def saves(source, tiles, out, sems, started):
+def saves(order, source, tiles, out, sems, started):
     def piece(first):
         def work():
-            restore(source, tiles, first)
+            restore(order, source, tiles, first)
             part = pl.ds(first, 512)
             copy = pltpu.make_async_copy(tiles.at[part], out.at[part], sems.at[first // 512])
             copy.start()
@@ -271,15 +291,31 @@
     return lambda r: ref[r]
 
 
-def first_last_layer(xt, last_weights, bias, cells, weights, gate_rows, memory, hidden, first_weights, shifted, sem):
+def first_last_layer(
+    xt, bias, cells, weights, _, gate_rows, memory, hidden, first_weights, last_weights, shifted, sems
+):
     layer = bias.shape[0] - 1
     channels = hidden.shape[1]
-    copy = pltpu.make_async_copy(weights.at[0], first_weights, sem)
-    copy.start()
+    half = channels // 2
+    copies = []
+    for q in range(4):
+        part = pl.ds(q * channels + half, half)
+        copies.append(pltpu.make_async_copy(weights.at[layer, part], last_weights.at[part], sems.at[q]))
+    copies.append(pltpu.make_async_copy(weights.at[0], first_weights, sems.at[4]))
+    for copy in copies:
+        copy.start()
+
+    def weights_of(low):
+        if low > 0:
+            for copy in copies[:4]:
+                copy.wait()
+        parts = [last_weights[q * channels + low : q * channels + low + half] for q in range(4)]
+        return jnp.concatenate(parts, axis=0)
+
     run_layer(
         (part_of(xt, layer - 1, channels), part_of(xt, layer, channels)),
         None,
-        last_weights[...],
+        weights_of,
         bias[layer],
         lambda at: cells[layer, at, :],
         memory,
@@ -287,7 +323,7 @@
         gate_rows,
         shifted,
     )
-    copy.wait()
+    copies[4].wait()
 
 
 def pack_kernel(rows, first_own, second_own, first_got, second_got, packed, sent, next_edge, taps, cell_edge):
@@ -300,6 +336,8 @@
     own_left = jnp.where(even, second_own[...], first_own[...])
     from_left = jnp.where(even, second_got[...], first_got[...])
     from_right = jnp.where(even, first_got[...], second_got[...])
+    from_left = jnp.where(tile_place() > 0, from_left, jnp.zeros_like(from_left))
+    from_right = jnp.where(tile_place() < GRID_COLS - 1, from_right, jnp.zeros_like(from_right))
     lane = iota((channels, LANES), 1)
 
     def laid(k, pieces):
@@ -360,6 +398,7 @@
     first = lax.axis_index("section") == 0
     rows, channels, _ = packet.shape
     layers = bias.shape[0]
+    order = swap_matrix(rows, 256 // rows, False)
     started = []
     edges = (jnp.where(first, packed[layers], packet_edge[...]), packed[0])
     run_layer(
@@ -372,7 +411,7 @@
         before,
         first_gates,
         shifted,
-        saves(gate_rows, tiles, gates.at[0, layers - 1], sems.at[0], started),
+        saves(order, gate_rows, tiles, gates.at[0, layers - 1], sems.at[0], started),
     )
     wide = jnp.concatenate(edges, axis=0)
     columns = [turned(wide, -2 * rows * b) for b in range(3)]
@@ -388,7 +427,7 @@
         next_hidden,
         next_gates,
         shifted,
-        saves(first_gates, other_tiles, gates.at[0, 0], sems.at[1], started),
+        saves(order, first_gates, other_tiles, gates.at[0, 0], sems.at[1], started),
     )
     for copy in started:
         copy.wait()
@@ -403,6 +442,7 @@
     rows = packet.shape[0] - 1
     channels = packet.shape[1]
     layer = bias.shape[0] - 1
+    order = swap_matrix(rows, 256 // rows, False)
     started = [pltpu.make_async_copy(last_memory, memory_out.at[layer], cell_sems.at[0])]
     started[0].start()
     frame = xt.shape[1] // channels - 1
@@ -416,15 +456,15 @@
         first_hidden,
         first_gates,
         shifted,
-        saves(last_gates, tiles, gates.at[1, layer], sems.at[0], started)
-        + saves(last_hidden, hidden_tiles, hidden_out.at[layer], sems.at[2], started),
+        saves(order, last_gates, tiles, gates.at[1, layer], sems.at[0], started)
+        + saves(order, last_hidden, hidden_tiles, hidden_out.at[layer], sems.at[2], started),
     )
     copy = pltpu.make_async_copy(first_memory, memory_out.at[0], cell_sems.at[1])
     copy.start()
     started.append(copy)
-    for work in saves(first_gates, other_tiles, gates.at[1, 0], sems.at[1], started):
+    for work in saves(order, first_gates, other_tiles, gates.at[1, 0], sems.at[1], started):
         work()
-    for work in saves(first_hidden, other_hidden, hidden_out.at[0], sems.at[3], started):
+    for work in saves(order, first_hidden, other_hidden, hidden_out.at[0], sems.at[3], started):
         work()
     for copy in started:
         copy.wait()
@@ -440,7 +480,7 @@
     weights, biases = in_hbm(weights), in_hbm(biases)
     plane = (channels, LANES)
     sections = lax.axis_size("section")
-    ahead = [(i, i + 1) for i in range(sections - 1)]
+    ahead = [(i, (i + 1) % sections) for i in range(sections)]
 
     def call(kernel, ins, outs, scratch=(), hbm=(), out_specs=None, aliases=None):
         return pl.pallas_call(
@@ -464,7 +504,7 @@
     hidden_tiles = pltpu.VMEM((flat, LANES), bf16)
     pieces = gate_count * rows // 512
 
-    xt, sent, first_edges, second_edges, cells, wide_bias, last_weights = call(
+    xt, sent, first_edges, second_edges, cells, wide_bias, half_weights = call(
         prep_kernel,
         (frames, hidden_init, memory_init, biases, weights),
         [
@@ -479,19 +519,20 @@
         [
             pltpu.VMEM((layers + steps, flat, LANES), bf16),
             pltpu.VMEM((layers, gate_count), f32),
-            pltpu.SemaphoreType.DMA((5,)),
+            pltpu.SemaphoreType.DMA((8,)),
         ],
         hbm=range(5),
     )
     packet = permuted(sent, "section", ahead)
     first_got = permuted(first_edges, "tile", swap_pairs(0))
     second_got = permuted(second_edges, "tile", swap_pairs(1))
-    rough_gates, rough_memory, rough_hidden, first_weights = call(
+    rough_gates, rough_memory, rough_hidden, first_weights, last_weights = call(
         first_last_layer,
-        (xt, last_weights, wide_bias, cells, weights),
-        [gate_rows, memory, state, layer_weights],
-        [shifted, pltpu.SemaphoreType.DMA],
-        hbm=(4,),
+        (xt, wide_bias, cells, weights, half_weights),
+        [gate_rows, memory, state, layer_weights, layer_weights],
+        [shifted, pltpu.SemaphoreType.DMA((5,))],
+        hbm=(3,),
+        aliases={4: 4},
     )
     packed, sent_edge, next_edge, taps, cell_edge = call(
         functools.partial(pack_kernel, rows),

time: 45.9 us -> 42.5 us (0.926)
  starting transfers between devices: 14.7 us -> 10.2 us
  waiting for transfers between devices: 9.21 us -> 11 us
  Pallas kernels: 20.9 us -> 20.2 us
    ppermute x5, starting transfers between devices: 14.7 us -> 10.2 us  [permuted(): return in_vmem(lax.ppermute(array, axis, pairs))]
    ppermute x5, waiting for transfers between devices: 9.21 us -> 11 us  [permuted(): return in_vmem(lax.ppermute(array, axis, pairs))]
    pallas_call x6, Pallas kernels: 20.9 us -> 20.2 us  [call(): pl.pallas_call(kernel, in_specs=[HBM if i in hbm else VMEM for i in range...]
  transfers between devices with their start and end apart: 5 -> 5, of which waited for: 1 -> 1; matrix products, arithmetic and copies ran while one was open for 0% -> 0% of each run, Pallas kernels for 24% -> 25%
where the time goes in v3:
time: 42.5 us; the launch traced here: 42.3 us
  Pallas kernels  20.2 us (48%)
  waiting for transfers between devices  11 us (26%)
  starting transfers between devices  10.2 us (24%)
  between operations  0.85 us (2%)
    pallas_call x6, Pallas kernels, call(): pl.pallas_call(kernel, in_specs=[HBM if i in hbm else VMEM for i in range...  20.2 us
    ppermute x5, waiting for transfers between devices, permuted(): return in_vmem(lax.ppermute(array, axis, pairs))  11 us
    ppermute x5, starting transfers between devices, permuted(): return in_vmem(lax.ppermute(array, axis, pairs))  10.2 us
  transfers between devices with their start and end apart: 5, of which 1 were waited for; matrix products, arithmetic and copies ran while one was open for 0% of the time, Pallas kernels for 25%

profile of v3, /device:TPU:0, one launch (start us, length us, event | category | flops | bytes accessed | tf_op | source)
XLA Modules:
  0.0 42.3 jit_solution(12250062563128929498)
XLA Ops:
  0.6 2.5 %shard_map.76 = (bf16[8,512,128]{2,1,0:T(8,128)(2,1)S(1)}, bf16[8,128,128]{2,1,0:T(8,128)(2,1)S(1)}, bf16[128,128]{1,0:T(8,128)(2,1)S(1)}, bf16[128,128]{1,0:T(8...) custom-call(bf16[2,1024,128]{2,1,0:T(8,128)(2,1)} %bitcast.14, ...), custom_call_target="tpu_custom_call" | custom-call | tf_op jit(solution)/shard_map/pallas_call | solution.py:486
  3.2 3.1 %collective-permute-start = (bf16[128,128]{1,0:T(8,128)(2,1)S(1)}, bf16[128,128]{1,0:T(8,128)(2,1)S(1)}, u32[]{:S(2)}, u32[]{:S(2)}) collective-permute-start(bf16[128,128]{1,0:T(8,128)(2,1)S(1)} %get-tuple-element.33.first_own), channel_id=1, source_target_pairs={{8,10},{10,8},{12,14},{14,12},{0,2},{2,0},{4,6},{6,4},{9,11},{11,9... | collective-permute-start | bytes 98312 | tf_op jit(solution)/shard_map/ppermute | solution.py:37
  6.2 3.6 %collective-permute-start.1 = (bf16[128,128]{1,0:T(8,128)(2,1)S(1)}, bf16[128,128]{1,0:T(8,128)(2,1)S(1)}, u32[]{:S(2)}, u32[]{:S(2)}) collective-permute-start(bf16[128,128]{1,0:T(8,128)(2,1)S(1)} %get-tuple-element.34.second_own), channel_id=1, source_target_pairs={{10,12},{12,10},{14,0},{0,14},{2,4},{4,2},{6,8},{8,6},{11,13},{13,... | collective-permute-start | bytes 98312 | tf_op jit(solution)/shard_map/ppermute | solution.py:37
  9.8 3.2 %shard_map.78 = (bf16[8,512,128]{2,1,0:T(8,128)(2,1)S(1)}, f32[1024,128]{1,0:T(8,128)S(1)}, bf16[8,128,128]{2,1,0:T(8,128)(2,1)S(1)}, bf16[512,2304]{1,0:T(8,128)(2,1)S(1)}, bf16[512,2304]{1,0:T(8,128)(2,1)S(1)}) custom-call(bf16[8,512,128]{2,1,0:T(8,128)(2,1)S(1)} %get-tuple-element.32.xt, ...), custom_call_target="tpu_custom_call", output_to_operand_aliasing={{4}: (4, {})} | custom-call | tf_op jit(solution)/shard_map/pallas_call | solution.py:486
  13.0 0.0 collective-permute-done.first_got
  13.0 0.0 collective-permute-done.1.second_got
  13.0 0.4 %shard_map.77 = (bf16[3,128,128]{2,1,0:T(8,128)(2,1)S(1)}, bf16[128,128]{1,0:T(8,128)(2,1)S(1)}, bf16[128,128]{1,0:T(8,128)(2,1)S(1)}, bf16[3,256,128]{2,1,0:T(8,128)(2,1)S(1)}, f32[2,128,128]{2,1,0:T(8,128)S(1)}) custom-call(bf16[128,128]{1,0:T(8,128)(2,1)S(1)} %get-tuple-element.33.first_own, bf16[128,128]{1,0:T(8,128)(2,1)S(1)} %get-tuple-element.34.second_own, ...), custom_call_target="tpu_custom_call" | custom-call | tf_op jit(solution)/shard_map/pallas_call | solution.py:486
  13.5 1.7 %shard_map.79 = (bf16[9,128,128]{2,1,0:T(8,128)(2,1)S(1)}, f32[1024,128]{1,0:T(8,128)S(1)}, bf16[8,512,128]{2,1,0:T(8,128)(2,1)S(1)}) custom-call(bf16[3,256,128]{2,1,0:T(8,128)(2,1)S(1)} %get-tuple-element.35.taps, bf16[512,2304]{1,0:T(8,128)(2,1)S(1)} %get-tuple-element.39.last_weights, f32[2,512,128]{2,1,0:T(8,128)S(1)} %get-tuple-element.36.bias, ...), custom_call_target="tpu_custom_call" | custom-call | tf_op jit(solution)/shard_map/pallas_call | solution.py:486
  15.1 1.5 %collective-permute-start.2 = (bf16[9,128,128]{2,1,0:T(8,128)(2,1)S(1)}, bf16[9,128,128]{2,1,0:T(8,128)(2,1)S(1)}, u32[]{:S(2)}, u32[]{:S(2)}) collective-permute-start(bf16[9,128,128]{2,1,0:T(8,128)(2,1)S(1)} %get-tuple-element.44.last), channel_id=1, source_target_pairs={{0,16},{16,0},{1,17},{17,1},{2,18},{18,2},{3,19},{19,3},{4,20},{20... | collective-permute-start | bytes 884744 | tf_op jit(solution)/shard_map/ppermute | solution.py:37
  16.7 0.5 %collective-permute-start.3 = (bf16[8,128,128]{2,1,0:T(8,128)(2,1)S(1)}, bf16[8,128,128]{2,1,0:T(8,128)(2,1)S(1)}, u32[]{:S(2)}, u32[]{:S(2)}) collective-permute-start(bf16[8,128,128]{2,1,0:T(8,128)(2,1)S(1)} %get-tuple-element.46), channel_id=1, source_target_pairs={{0,16},{16,0},{1,17},{17,1},{2,18},{18,2},{3,19},{19,3},{4,20},{20... | collective-permute-start | bytes 786440 | tf_op jit(solution)/shard_map/ppermute | solution.py:37
  17.2 1.5 %collective-permute-start.4 = (bf16[128,128]{1,0:T(8,128)(2,1)S(1)}, bf16[128,128]{1,0:T(8,128)(2,1)S(1)}, u32[]{:S(2)}, u32[]{:S(2)}) collective-permute-start(bf16[128,128]{1,0:T(8,128)(2,1)S(1)} %get-tuple-element.47), channel_id=1, source_target_pairs={{0,16},{16,0},{1,17},{17,1},{2,18},{18,2},{3,19},{19,3},{4,20},{20... | collective-permute-start | bytes 98312 | tf_op jit(solution)/shard_map/ppermute | solution.py:37
  18.7 11.0 %collective-permute-done.4.packet_edge = bf16[128,128]{1,0:T(8,128)(2,1)S(1)} collective-permute-done((bf16[128,128]{1,0:T(8,128)(2,1)S(1)}, bf16[128,128]{1,0:T(8,128)(2,1)S(1)}, u32[]{:S(2)}, u32[]{:S(2)}) %collective-permute-start.4) | collective-permute-done | bytes 32800 | tf_op jit(solution)/shard_map/ppermute | solution.py:37
  29.7 0.0 collective-permute-done.3.packet
  29.7 7.1 %shard_map.80 = (bf16[9,128,128]{2,1,0:T(8,128)(2,1)S(1)}, f32[1024,128]{1,0:T(8,128)S(1)}, bf16[8,512,128]{2,1,0:T(8,128)(2,1)S(1)}, f32[1024,128]{1,0:T(8,128)...) custom-call(bf16[8,512,128]{2,1,0:T(8,128)(2,1)S(1)} %get-tuple-element.32.xt, ...), custom_call_target="tpu_custom_call" | custom-call | tf_op jit(solution)/shard_map/pallas_call | solution.py:486
  36.9 0.0 collective-permute-done.2.packet
  36.9 5.2 %shard_map.81 = (bf16[2,2,4096,128]{3,2,1,0:T(8,128)(2,1)}, bf16[2,1024,128]{2,1,0:T(8,128)(2,1)}, f32[2,1024,128]{2,1,0:T(8,128)}) custom-call(bf16[8,512,128]{2,1,0:T(8,128)(2,1)S(1)} %get-tuple-element.32.xt, bf16[9,128,128]{2,1,0:T(8,128)(2,1)S(1)} %collective-permute-done.2.packet, ...), custom_call_target="tpu_custom_call", output_to_operand_aliasing={{0}: (10, {})} | custom-call | tf_op jit(solution)/shard_map/pallas_call | solution.py:486
Async XLA Ops:
  3.2 9.9 %collective-permute-start = (bf16[128,128]{1,0:T(8,128)(2,1)S(1)}, bf16[128,128]{1,0:T(8,128)(2,1)S(1)}, u32[]{:S(2)}, u32[]{:S(2)}) collective-permute-start(bf16[128,128]{1,0:T(8,128)(2,1)S(1)} %get-tuple-element.33.first_own), channel_id=1, source_target_pairs={{8,10},{10,8},{12,14},{14,12},{0,2},{2,0},{4,6},{6,4},{9,11},{11,9... | collective-permute-start | bytes 98312 | tf_op jit(solution)/shard_map/ppermute | solution.py:37
  6.2 6.8 %collective-permute-start.1 = (bf16[128,128]{1,0:T(8,128)(2,1)S(1)}, bf16[128,128]{1,0:T(8,128)(2,1)S(1)}, u32[]{:S(2)}, u32[]{:S(2)}) collective-permute-start(bf16[128,128]{1,0:T(8,128)(2,1)S(1)} %get-tuple-element.34.second_own), channel_id=1, source_target_pairs={{10,12},{12,10},{14,0},{0,14},{2,4},{4,2},{6,8},{8,6},{11,13},{13,... | collective-permute-start | bytes 98312 | tf_op jit(solution)/shard_map/ppermute | solution.py:37
  15.1 21.7 %collective-permute-start.2 = (bf16[9,128,128]{2,1,0:T(8,128)(2,1)S(1)}, bf16[9,128,128]{2,1,0:T(8,128)(2,1)S(1)}, u32[]{:S(2)}, u32[]{:S(2)}) collective-permute-start(bf16[9,128,128]{2,1,0:T(8,128)(2,1)S(1)} %get-tuple-element.44.last), channel_id=1, source_target_pairs={{0,16},{16,0},{1,17},{17,1},{2,18},{18,2},{3,19},{19,3},{4,20},{20... | collective-permute-start | bytes 884744 | tf_op jit(solution)/shard_map/ppermute | solution.py:37
  16.7 13.0 %collective-permute-start.3 = (bf16[8,128,128]{2,1,0:T(8,128)(2,1)S(1)}, bf16[8,128,128]{2,1,0:T(8,128)(2,1)S(1)}, u32[]{:S(2)}, u32[]{:S(2)}) collective-permute-start(bf16[8,128,128]{2,1,0:T(8,128)(2,1)S(1)} %get-tuple-element.46), channel_id=1, source_target_pairs={{0,16},{16,0},{1,17},{17,1},{2,18},{18,2},{3,19},{19,3},{4,20},{20... | collective-permute-start | bytes 786440 | tf_op jit(solution)/shard_map/ppermute | solution.py:37
  17.2 12.5 %collective-permute-start.4 = (bf16[128,128]{1,0:T(8,128)(2,1)S(1)}, bf16[128,128]{1,0:T(8,128)(2,1)S(1)}, u32[]{:S(2)}, u32[]{:S(2)}) collective-permute-start(bf16[128,128]{1,0:T(8,128)(2,1)S(1)} %get-tuple-element.47), channel_id=1, source_target_pairs={{0,16},{16,0},{1,17},{17,1},{2,18},{18,2},{3,19},{19,3},{4,20},{20... | collective-permute-start | bytes 98312 | tf_op jit(solution)/shard_map/ppermute | solution.py:37

commit v4 on v3

--- a/solution.py
+++ b/solution.py
@@ -71,7 +71,7 @@
 
 
 def prep_kernel(
-    frames, hidden, memory, bias, weights, xt, sent, first_edges, second_edges, cells, wide_bias, half_weights,
+    frames, hidden, memory, bias, weights, xt, sent, first_edges, second_edges, cells, wide_bias, last_weights,
     raw, raw_bias, sems,
 ):
     layers, _, _ = hidden.shape
@@ -82,10 +82,7 @@
         pltpu.make_async_copy(memory, cells, sems.at[2]),
         pltpu.make_async_copy(bias, raw_bias, sems.at[3]),
     ]
-    half = channels // 2
-    for q in range(4):
-        source = weights.at[layers - 1, pl.ds(q * channels, half)]
-        copies.append(pltpu.make_async_copy(source, half_weights.at[pl.ds(q * channels, half)], sems.at[4 + q]))
+    copies.append(pltpu.make_async_copy(weights.at[layers - 1], last_weights, sems.at[4]))
     copies[3].start()
     for copy in copies[:3] + copies[4:]:
         copy.start()
@@ -150,8 +147,7 @@
     even = tile_place() % 2 == 0
     first_edges[...] = jnp.where(even, right, left).astype(bf16)
     second_edges[...] = jnp.where(even, left, right).astype(bf16)
-    for copy in copies[4:]:
-        copy.wait()
+    copies[4].wait()
 
 
 def cell_step(pre, bias, memory):
@@ -193,9 +189,7 @@
 
     for r in range(rows):
         build(r)
-    beside = list(beside)
     tiles = rows // 2
-    share = -(-len(beside) // tiles)
     parts = 1 if beside else 2
     size = channels // parts
     for low in range(0, channels, size):
@@ -206,7 +200,7 @@
             part_weights = weights(low)
             part_bias = jnp.concatenate([bias[c] for c in chosen], axis=0)
         for j in range(tiles):
-            for work in beside[j * share : (j + 1) * share]:
+            for work in beside[j] if beside else ():
                 work()
             patches = jnp.concatenate(
                 [
@@ -273,6 +267,17 @@
     return [piece(first) for first in range(0, tiles.shape[0], 512)]
 
 
+def dealt(works, hands):
+    share = -(-len(works) // hands)
+    return [works[j * share : (j + 1) * share] for j in range(hands)]
+
+
+def mended(value, column, r, rows):
+    lane = iota(value.shape, 1)
+    value = jnp.where(lane == 0, turned(column, -2 * rows - r), value)
+    return jnp.where(lane == LANES - 1, turned(column, -1 - 3 * rows - r), value)
+
+
 def part_of(ref, k, channels):
     def load(r):
         return ref[r, k * channels : (k + 1) * channels]
@@ -291,31 +296,15 @@
     return lambda r: ref[r]
 
 
-def first_last_layer(
-    xt, bias, cells, weights, _, gate_rows, memory, hidden, first_weights, last_weights, shifted, sems
-):
+def first_last_layer(xt, bias, cells, weights, last_weights, gate_rows, memory, hidden, first_weights, shifted, sem):
     layer = bias.shape[0] - 1
     channels = hidden.shape[1]
-    half = channels // 2
-    copies = []
-    for q in range(4):
-        part = pl.ds(q * channels + half, half)
-        copies.append(pltpu.make_async_copy(weights.at[layer, part], last_weights.at[part], sems.at[q]))
-    copies.append(pltpu.make_async_copy(weights.at[0], first_weights, sems.at[4]))
-    for copy in copies:
-        copy.start()
-
-    def weights_of(low):
-        if low > 0:
-            for copy in copies[:4]:
-                copy.wait()
-        parts = [last_weights[q * channels + low : q * channels + low + half] for q in range(4)]
-        return jnp.concatenate(parts, axis=0)
-
+    copy = pltpu.make_async_copy(weights.at[0], first_weights, sem)
+    copy.start()
     run_layer(
         (part_of(xt, layer - 1, channels), part_of(xt, layer, channels)),
         None,
-        weights_of,
+        lambda low: halved(last_weights, low),
         bias[layer],
         lambda at: cells[layer, at, :],
         memory,
@@ -323,7 +312,7 @@
         gate_rows,
         shifted,
     )
-    copies[4].wait()
+    copy.wait()
 
 
 def pack_kernel(rows, first_own, second_own, first_got, second_got, packed, sent, next_edge, taps, cell_edge):
@@ -368,55 +357,71 @@
         cell_edge[k] = high.astype(f32) + low.astype(f32)
 
 
-def mend_kernel(taps, last_weights, bias, cell_edge, gate_rows, memory, hidden, last, new_memory, new_gates):
+def mend_kernel(taps, last_weights, bias, cell_edge, hidden, last, edge_memory, edge_gates):
     rows, channels, _ = hidden.shape
     layer = bias.shape[0] - 1
-    gates, edge_memory, edge_hidden = edge_step(
+    gates, memory, edge_hidden = edge_step(
         [taps[b] for b in range(3)], last_weights[...], bias[layer], cell_edge[layer], rows
     )
     last[rows] = outer_columns(edge_hidden, rows)
-    gates = jnp.concatenate([gate.astype(bf16) for gate in gates], axis=0)
-
-    def mended(value, column, r):
-        lane = iota(value.shape, 1)
-        value = jnp.where(lane == 0, turned(column, -2 * rows - r), value)
-        return jnp.where(lane == LANES - 1, turned(column, -1 - 3 * rows - r), value)
-
     for r in range(rows):
-        last[r] = mended(hidden[r], edge_hidden, r)
+        last[r] = mended(hidden[r], edge_hidden, r, rows)
+    edge_memory[...] = memory
+    for q in range(4):
+        edge_gates[q * channels : (q + 1) * channels] = gates[q].astype(bf16)
+
+
+def halved(weights, low):
+    channels = weights.shape[0] // 4
+    parts = [weights[q * channels + low : q * channels + low + channels // 2] for q in range(4)]
+    return jnp.concatenate(parts, axis=0)
+
+
+def settle_kernel(rough_gates, rough_memory, edge_gates, edge_memory, last_memory, last_tiles, last_gates):
+    rows, gate_count, _ = rough_gates.shape
+    channels = gate_count // 4
+    order = swap_matrix(rows, 256 // rows, False)
+    for r in range(rows):
+        last_gates[r] = mended(rough_gates[r], edge_gates[...], r, rows)
+    for first in range(0, last_tiles.shape[0], 512):
+        restore(order, last_gates, last_tiles, first)
     for r in range(rows):
         at = pl.ds(r, channels, stride=rows)
-        new_memory[at, :] = mended(memory[at, :], edge_memory, r)
-        new_gates[r] = mended(gate_rows[r], gates, r)
+        last_memory[at, :] = mended(rough_memory[at, :], edge_memory[...], r, rows)
 
 
 def middle_kernel(
-    xt, packet, packet_edge, packed, first_weights, last_weights, bias, cells, cell_edge, gate_rows, last, last_memory,
+    xt, packet, packet_edge, packed, first_weights, last_weights, bias, cells, cell_edge,
+    last, last_memory, last_tiles,
     before, before_memory, next_gates, next_memory, next_hidden, gates,
-    shifted, first_gates, tiles, other_tiles, sems,
+    shifted, first_gates, tiles, sems, last_sem,
 ):
     first = lax.axis_index("section") == 0
     rows, channels, _ = packet.shape
     layers = bias.shape[0]
     order = swap_matrix(rows, 256 // rows, False)
-    started = []
+    started = [pltpu.make_async_copy(last_tiles, gates.at[0, layers - 1], last_sem)]
+    started[0].start()
     edges = (jnp.where(first, packed[layers], packet_edge[...]), packed[0])
+
+    def outside():
+        wide = jnp.concatenate(edges, axis=0)
+        columns = [turned(wide, -2 * rows * b) for b in range(3)]
+        _, _, hidden = edge_step(columns, first_weights[...], bias[0], cell_edge[0], rows)
+        before[rows] = outer_columns(hidden, rows)
+
     run_layer(
         (either(first, part_of(xt, layers, channels), whole(packet)), part_of(xt, 0, channels)),
         edges,
-        first_weights[...],
+        lambda low: halved(first_weights, low),
         bias[0],
         lambda at: cells[0, at, :],
         before_memory,
         before,
         first_gates,
         shifted,
-        saves(order, gate_rows, tiles, gates.at[0, layers - 1], sems.at[0], started),
-    )
-    wide = jnp.concatenate(edges, axis=0)
-    columns = [turned(wide, -2 * rows * b) for b in range(3)]
-    _, _, hidden = edge_step(columns, first_weights[...], bias[0], cell_edge[0], rows)
-    before[rows] = outer_columns(hidden, rows)
+    )
+    outside()
     run_layer(
         (whole(before), whole(last)),
         (before[rows], last[rows]),
@@ -427,7 +432,7 @@
         next_hidden,
         next_gates,
         shifted,
-        saves(order, first_gates, other_tiles, gates.at[0, 0], sems.at[1], started),
+        dealt(saves(order, first_gates, tiles, gates.at[0, 0], sems, started), rows // 2),
     )
     for copy in started:
         copy.wait()
@@ -446,18 +451,20 @@
     started = [pltpu.make_async_copy(last_memory, memory_out.at[layer], cell_sems.at[0])]
     started[0].start()
     frame = xt.shape[1] // channels - 1
+    for work in saves(order, last_gates, tiles, gates.at[1, layer], sems.at[0], started):
+        work()
+    for work in saves(order, last_hidden, hidden_tiles, hidden_out.at[layer], sems.at[2], started):
+        work()
     run_layer(
         (either(first, part_of(xt, frame, channels), whole(packet)), whole(before)),
         (jnp.where(first, next_edge[...], packet[rows]), before[rows]),
-        first_weights[...],
+        lambda low: halved(first_weights, low),
         bias[0],
         lambda at: before_memory[at, :],
         first_memory,
         first_hidden,
         first_gates,
         shifted,
-        saves(order, last_gates, tiles, gates.at[1, layer], sems.at[0], started)
-        + saves(order, last_hidden, hidden_tiles, hidden_out.at[layer], sems.at[2], started),
     )
     copy = pltpu.make_async_copy(first_memory, memory_out.at[0], cell_sems.at[1])
     copy.start()
@@ -504,7 +511,7 @@
     hidden_tiles = pltpu.VMEM((flat, LANES), bf16)
     pieces = gate_count * rows // 512
 
-    xt, sent, first_edges, second_edges, cells, wide_bias, half_weights = call(
+    xt, sent, first_edges, second_edges, cells, wide_bias, last_weights = call(
         prep_kernel,
         (frames, hidden_init, memory_init, biases, weights),
         [
@@ -519,20 +526,19 @@
         [
             pltpu.VMEM((layers + steps, flat, LANES), bf16),
             pltpu.VMEM((layers, gate_count), f32),
-            pltpu.SemaphoreType.DMA((8,)),
+            pltpu.SemaphoreType.DMA((5,)),
         ],
         hbm=range(5),
     )
     packet = permuted(sent, "section", ahead)
     first_got = permuted(first_edges, "tile", swap_pairs(0))
     second_got = permuted(second_edges, "tile", swap_pairs(1))
-    rough_gates, rough_memory, rough_hidden, first_weights, last_weights = call(
+    rough_gates, rough_memory, rough_hidden, first_weights = call(
         first_last_layer,
-        (xt, wide_bias, cells, weights, half_weights),
-        [gate_rows, memory, state, layer_weights, layer_weights],
-        [shifted, pltpu.SemaphoreType.DMA((5,))],
+        (xt, wide_bias, cells, weights, last_weights),
+        [gate_rows, memory, state, layer_weights],
+        [shifted, pltpu.SemaphoreType.DMA],
         hbm=(3,),
-        aliases={4: 4},
     )
     packed, sent_edge, next_edge, taps, cell_edge = call(
         functools.partial(pack_kernel, rows),
@@ -546,21 +552,27 @@
         ],
     )
     packet_edge = permuted(sent_edge, "section", ahead)
-    last, last_memory, last_gates = call(
+    last, edge_memory, edge_gates = call(
         mend_kernel,
-        (taps, last_weights, wide_bias, cell_edge, rough_gates, rough_memory, rough_hidden),
-        [state_and_edge, memory, gate_rows],
+        (taps, last_weights, wide_bias, cell_edge, rough_hidden),
+        [state_and_edge, pltpu.VMEM(plane, f32), pltpu.VMEM((gate_count, LANES), bf16)],
     )
     next_packet = permuted(last, "section", ahead)
     gates_shape = jax.ShapeDtypeStruct((steps, layers, gate_count * rows, LANES), bf16)
+    last_memory, last_tiles = call(
+        settle_kernel,
+        (rough_gates, rough_memory, edge_gates, edge_memory),
+        [memory, gate_tiles],
+        [gate_rows],
+    )
     before, before_memory, next_gates, next_memory, next_hidden, gates = call(
         middle_kernel,
         (
             xt, packet, packet_edge, packed, first_weights, last_weights, wide_bias, cells, cell_edge,
-            last_gates, last, last_memory,
+            last, last_memory, last_tiles,
         ),
         [state_and_edge, memory, gate_rows, memory, state, gates_shape],
-        [shifted, gate_rows, gate_tiles, gate_tiles, pltpu.SemaphoreType.DMA((2, pieces))],
+        [shifted, gate_rows, gate_tiles, pltpu.SemaphoreType.DMA((pieces,)), pltpu.SemaphoreType.DMA],
         out_specs=[VMEM] * 5 + [HBM],
     )
     gates, hidden_out, memory_out = call(

time: 42.5 us -> 41.1 us (0.967)
  waiting for transfers between devices: 11 us -> 9.98 us
    ppermute x5, waiting for transfers between devices: 11 us -> 9.98 us  [permuted(): return in_vmem(lax.ppermute(array, axis, pairs))]
    pallas_call x6 -> x7, Pallas kernels: 20.2 us -> 19.9 us  [call(): pl.pallas_call(kernel, in_specs=[HBM if i in hbm else VMEM for i in range...]
  transfers between devices with their start and end apart: 5 -> 5, of which waited for: 1 -> 2; matrix products, arithmetic and copies ran while one was open for 0% -> 0% of each run, Pallas kernels for 25% -> 26%
where the time goes in v4:
time: 41.1 us; the launch traced here: 41 us
  Pallas kernels  19.9 us (48%)
  starting transfers between devices  10.2 us (25%)
  waiting for transfers between devices  9.98 us (24%)
  between operations  0.86 us (2%)
    pallas_call x7, Pallas kernels, call(): pl.pallas_call(kernel, in_specs=[HBM if i in hbm else VMEM for i in range...  19.9 us
    ppermute x5, starting transfers between devices, permuted(): return in_vmem(lax.ppermute(array, axis, pairs))  10.2 us
    ppermute x5, waiting for transfers between devices, permuted(): return in_vmem(lax.ppermute(array, axis, pairs))  9.98 us
  transfers between devices with their start and end apart: 5, of which 2 were waited for; matrix products, arithmetic and copies ran while one was open for 0% of the time, Pallas kernels for 26%

profile of v4, /device:TPU:0, one launch (start us, length us, event | category | flops | bytes accessed | tf_op | source)
XLA Modules:
  0.0 41.0 jit_solution(1733818719788364188)
XLA Ops:
  0.6 2.5 %shard_map.76 = (bf16[8,512,128]{2,1,0:T(8,128)(2,1)S(1)}, bf16[8,128,128]{2,1,0:T(8,128)(2,1)S(1)}, bf16[128,128]{1,0:T(8,128)(2,1)S(1)}, bf16[128,128]{1,0:T(8...) custom-call(bf16[2,1024,128]{2,1,0:T(8,128)(2,1)} %bitcast.14, ...), custom_call_target="tpu_custom_call" | custom-call | tf_op jit(solution)/shard_map/pallas_call | solution.py:493
  3.1 3.1 %collective-permute-start = (bf16[128,128]{1,0:T(8,128)(2,1)S(1)}, bf16[128,128]{1,0:T(8,128)(2,1)S(1)}, u32[]{:S(2)}, u32[]{:S(2)}) collective-permute-start(bf16[128,128]{1,0:T(8,128)(2,1)S(1)} %get-tuple-element.34.first_own), channel_id=1, source_target_pairs={{8,10},{10,8},{12,14},{14,12},{0,2},{2,0},{4,6},{6,4},{9,11},{11,9... | collective-permute-start | bytes 98312 | tf_op jit(solution)/shard_map/ppermute | solution.py:37
  6.2 3.6 %collective-permute-start.1 = (bf16[128,128]{1,0:T(8,128)(2,1)S(1)}, bf16[128,128]{1,0:T(8,128)(2,1)S(1)}, u32[]{:S(2)}, u32[]{:S(2)}) collective-permute-start(bf16[128,128]{1,0:T(8,128)(2,1)S(1)} %get-tuple-element.35.second_own), channel_id=1, source_target_pairs={{10,12},{12,10},{14,0},{0,14},{2,4},{4,2},{6,8},{8,6},{11,13},{13,... | collective-permute-start | bytes 98312 | tf_op jit(solution)/shard_map/ppermute | solution.py:37
  9.7 3.0 %shard_map.78 = (bf16[8,512,128]{2,1,0:T(8,128)(2,1)S(1)}, f32[1024,128]{1,0:T(8,128)S(1)}, bf16[8,128,128]{2,1,0:T(8,128)(2,1)S(1)}, bf16[512,2304]{1,0:T(8,128)(2,1)S(1)}) custom-call(bf16[8,512,128]{2,1,0:T(8,128)(2,1)S(1)} %get-tuple-element.33.xt, f32[2,512,128]{2,1,0:T(8,128)S(1)} %get-tuple-element.38.bias, ...), custom_call_target="tpu_custom_call" | custom-call | tf_op jit(solution)/shard_map/pallas_call | solution.py:493
  12.7 0.0 collective-permute-done.first_got
  12.7 0.1 collective-permute-done.1.second_got
  12.8 0.4 %shard_map.77 = (bf16[3,128,128]{2,1,0:T(8,128)(2,1)S(1)}, bf16[128,128]{1,0:T(8,128)(2,1)S(1)}, bf16[128,128]{1,0:T(8,128)(2,1)S(1)}, bf16[3,256,128]{2,1,0:T(8,128)(2,1)S(1)}, f32[2,128,128]{2,1,0:T(8,128)S(1)}) custom-call(bf16[128,128]{1,0:T(8,128)(2,1)S(1)} %get-tuple-element.34.first_own, bf16[128,128]{1,0:T(8,128)(2,1)S(1)} %get-tuple-element.35.second_own, ...), custom_call_target="tpu_custom_call" | custom-call | tf_op jit(solution)/shard_map/pallas_call | solution.py:493
  13.2 1.0 %shard_map.79 = (bf16[9,128,128]{2,1,0:T(8,128)(2,1)S(1)}, f32[128,128]{1,0:T(8,128)S(1)}, bf16[512,128]{1,0:T(8,128)(2,1)S(1)}) custom-call(bf16[3,256,128]{2,1,0:T(8,128)(2,1)S(1)} %get-tuple-element.36.taps, bf16[512,2304]{1,0:T(8,128)(2,1)S(1)} %get-tuple-element.37.last_weights, f32[2,512,128]{2,1,0:T(8,128)S(1)} %get-tuple-element.38.bias, ...), custom_call_target="tpu_custom_call" | custom-call | tf_op jit(solution)/shard_map/pallas_call | solution.py:493
  14.3 1.6 %collective-permute-start.2 = (bf16[9,128,128]{2,1,0:T(8,128)(2,1)S(1)}, bf16[9,128,128]{2,1,0:T(8,128)(2,1)S(1)}, u32[]{:S(2)}, u32[]{:S(2)}) collective-permute-start(bf16[9,128,128]{2,1,0:T(8,128)(2,1)S(1)} %get-tuple-element.42.last), channel_id=1, source_target_pairs={{0,16},{16,0},{1,17},{17,1},{2,18},{18,2},{3,19},{19,3},{4,20},{20... | collective-permute-start | bytes 884744 | tf_op jit(solution)/shard_map/ppermute | solution.py:37
  15.8 0.5 %collective-permute-start.3 = (bf16[8,128,128]{2,1,0:T(8,128)(2,1)S(1)}, bf16[8,128,128]{2,1,0:T(8,128)(2,1)S(1)}, u32[]{:S(2)}, u32[]{:S(2)}) collective-permute-start(bf16[8,128,128]{2,1,0:T(8,128)(2,1)S(1)} %get-tuple-element.44), channel_id=1, source_target_pairs={{0,16},{16,0},{1,17},{17,1},{2,18},{18,2},{3,19},{19,3},{4,20},{20... | collective-permute-start | bytes 786440 | tf_op jit(solution)/shard_map/ppermute | solution.py:37
  16.4 1.5 %collective-permute-start.4 = (bf16[128,128]{1,0:T(8,128)(2,1)S(1)}, bf16[128,128]{1,0:T(8,128)(2,1)S(1)}, u32[]{:S(2)}, u32[]{:S(2)}) collective-permute-start(bf16[128,128]{1,0:T(8,128)(2,1)S(1)} %get-tuple-element.45), channel_id=1, source_target_pairs={{0,16},{16,0},{1,17},{17,1},{2,18},{18,2},{3,19},{19,3},{4,20},{20... | collective-permute-start | bytes 98312 | tf_op jit(solution)/shard_map/ppermute | solution.py:37
  17.8 1.0 %shard_map.80 = (f32[1024,128]{1,0:T(8,128)S(1)}, bf16[4096,128]{1,0:T(8,128)(2,1)S(1)}) custom-call(bf16[8,512,128]{2,1,0:T(8,128)(2,1)S(1)} %get-tuple-element.48.rough_gates, f32[1024,128]{1,0:T(8,128)S(1)} %get-tuple-element.49.rough_memory, bf16[512,128]{1,0:T(8,128)(2,1)S(1)} %get-tuple-element.50.edge_gates, f32[128,128]{1,0:T(8,128)S(1)} %get-tuple-element.51.edge_memory), custom_call_target="tpu_custom_call" | custom-call | tf_op jit(solution)/shard_map/pallas_call | solution.py:493
  18.9 9.9 %collective-permute-done.4.packet_edge = bf16[128,128]{1,0:T(8,128)(2,1)S(1)} collective-permute-done((bf16[128,128]{1,0:T(8,128)(2,1)S(1)}, bf16[128,128]{1,0:T(8,128)(2,1)S(1)}, u32[]{:S(2)}, u32[]{:S(2)}) %collective-permute-start.4) | collective-permute-done | bytes 32800 | tf_op jit(solution)/shard_map/ppermute | solution.py:37
  28.8 0.0 collective-permute-done.3.packet
  28.8 6.8 %shard_map.81 = (bf16[9,128,128]{2,1,0:T(8,128)(2,1)S(1)}, f32[1024,128]{1,0:T(8,128)S(1)}, bf16[8,512,128]{2,1,0:T(8,128)(2,1)S(1)}, f32[1024,128]{1,0:T(8,128)...) custom-call(bf16[8,512,128]{2,1,0:T(8,128)(2,1)S(1)} %get-tuple-element.33.xt, ...), custom_call_target="tpu_custom_call" | custom-call | tf_op jit(solution)/shard_map/pallas_call | solution.py:493
  35.6 0.0 collective-permute-done.2.packet
  35.6 5.2 %shard_map.82 = (bf16[2,2,4096,128]{3,2,1,0:T(8,128)(2,1)}, bf16[2,1024,128]{2,1,0:T(8,128)(2,1)}, f32[2,1024,128]{2,1,0:T(8,128)}) custom-call(bf16[8,512,128]{2,1,0:T(8,128)(2,1)S(1)} %get-tuple-element.33.xt, bf16[9,128,128]{2,1,0:T(8,128)(2,1)S(1)} %collective-permute-done.2.packet, ...), custom_call_target="tpu_custom_call", output_to_operand_aliasing={{0}: (10, {})} | custom-call | tf_op jit(solution)/shard_map/pallas_call | solution.py:493
Async XLA Ops:
  3.1 9.6 %collective-permute-start = (bf16[128,128]{1,0:T(8,128)(2,1)S(1)}, bf16[128,128]{1,0:T(8,128)(2,1)S(1)}, u32[]{:S(2)}, u32[]{:S(2)}) collective-permute-start(bf16[128,128]{1,0:T(8,128)(2,1)S(1)} %get-tuple-element.34.first_own), channel_id=1, source_target_pairs={{8,10},{10,8},{12,14},{14,12},{0,2},{2,0},{4,6},{6,4},{9,11},{11,9... | collective-permute-start | bytes 98312 | tf_op jit(solution)/shard_map/ppermute | solution.py:37
  6.2 6.6 %collective-permute-start.1 = (bf16[128,128]{1,0:T(8,128)(2,1)S(1)}, bf16[128,128]{1,0:T(8,128)(2,1)S(1)}, u32[]{:S(2)}, u32[]{:S(2)}) collective-permute-start(bf16[128,128]{1,0:T(8,128)(2,1)S(1)} %get-tuple-element.35.second_own), channel_id=1, source_target_pairs={{10,12},{12,10},{14,0},{0,14},{2,4},{4,2},{6,8},{8,6},{11,13},{13,... | collective-permute-start | bytes 98312 | tf_op jit(solution)/shard_map/ppermute | solution.py:37
  14.3 21.3 %collective-permute-start.2 = (bf16[9,128,128]{2,1,0:T(8,128)(2,1)S(1)}, bf16[9,128,128]{2,1,0:T(8,128)(2,1)S(1)}, u32[]{:S(2)}, u32[]{:S(2)}) collective-permute-start(bf16[9,128,128]{2,1,0:T(8,128)(2,1)S(1)} %get-tuple-element.42.last), channel_id=1, source_target_pairs={{0,16},{16,0},{1,17},{17,1},{2,18},{18,2},{3,19},{19,3},{4,20},{20... | collective-permute-start | bytes 884744 | tf_op jit(solution)/shard_map/ppermute | solution.py:37
  15.8 13.0 %collective-permute-start.3 = (bf16[8,128,128]{2,1,0:T(8,128)(2,1)S(1)}, bf16[8,128,128]{2,1,0:T(8,128)(2,1)S(1)}, u32[]{:S(2)}, u32[]{:S(2)}) collective-permute-start(bf16[8,128,128]{2,1,0:T(8,128)(2,1)S(1)} %get-tuple-element.44), channel_id=1, source_target_pairs={{0,16},{16,0},{1,17},{17,1},{2,18},{18,2},{3,19},{19,3},{4,20},{20... | collective-permute-start | bytes 786440 | tf_op jit(solution)/shard_map/ppermute | solution.py:37
  16.4 12.4 %collective-permute-start.4 = (bf16[128,128]{1,0:T(8,128)(2,1)S(1)}, bf16[128,128]{1,0:T(8,128)(2,1)S(1)}, u32[]{:S(2)}, u32[]{:S(2)}) collective-permute-start(bf16[128,128]{1,0:T(8,128)(2,1)S(1)} %get-tuple-element.45), channel_id=1, source_target_pairs={{0,16},{16,0},{1,17},{17,1},{2,18},{18,2},{3,19},{19,3},{4,20},{20... | collective-permute-start | bytes 98312 | tf_op jit(solution)/shard_map/ppermute | solution.py:37

commit v5 on v4

--- a/solution.py
+++ b/solution.py
@@ -451,27 +451,28 @@
     started = [pltpu.make_async_copy(last_memory, memory_out.at[layer], cell_sems.at[0])]
     started[0].start()
     frame = xt.shape[1] // channels - 1
-    for work in saves(order, last_gates, tiles, gates.at[1, layer], sems.at[0], started):
-        work()
-    for work in saves(order, last_hidden, hidden_tiles, hidden_out.at[layer], sems.at[2], started):
-        work()
     run_layer(
         (either(first, part_of(xt, frame, channels), whole(packet)), whole(before)),
         (jnp.where(first, next_edge[...], packet[rows]), before[rows]),
-        lambda low: halved(first_weights, low),
+        first_weights[...],
         bias[0],
         lambda at: before_memory[at, :],
         first_memory,
         first_hidden,
         first_gates,
         shifted,
+        dealt(
+            saves(order, last_gates, tiles, gates.at[1, layer], sems.at[0], started)
+            + saves(order, last_hidden, hidden_tiles, hidden_out.at[layer], sems.at[2], started),
+            rows // 2,
+        ),
     )
     copy = pltpu.make_async_copy(first_memory, memory_out.at[0], cell_sems.at[1])
     copy.start()
     started.append(copy)
+    for work in saves(order, first_hidden, other_hidden, hidden_out.at[0], sems.at[3], started):
+        work()
     for work in saves(order, first_gates, other_tiles, gates.at[1, 0], sems.at[1], started):
-        work()
-    for work in saves(order, first_hidden, other_hidden, hidden_out.at[0], sems.at[3], started):
         work()
     for copy in started:
         copy.wait()

time: 41.1 us -> 41.1 us (level)
  no operation moved by 1% of the time
where the time goes in v5:
time: 41.1 us; the launch traced here: 40.9 us
  Pallas kernels  19.9 us (48%)
  starting transfers between devices  10.2 us (25%)
  waiting for transfers between devices  9.98 us (24%)
  between operations  0.86 us (2%)
    pallas_call x7, Pallas kernels, call(): pl.pallas_call(kernel, in_specs=[HBM if i in hbm else VMEM for i in range...  19.9 us
    ppermute x5, starting transfers between devices, permuted(): return in_vmem(lax.ppermute(array, axis, pairs))  10.2 us
    ppermute x5, waiting for transfers between devices, permuted(): return in_vmem(lax.ppermute(array, axis, pairs))  9.98 us
  transfers between devices with their start and end apart: 5, of which 2 were waited for; matrix products, arithmetic and copies ran while one was open for 0% of the time, Pallas kernels for 26%

profile of v5, /device:TPU:0, one launch (start us, length us, event | category | flops | bytes accessed | tf_op | source)
XLA Modules:
  0.0 40.9 jit_solution(9881551455786502960)
XLA Ops:
  0.6 2.5 %shard_map.76 = (bf16[8,512,128]{2,1,0:T(8,128)(2,1)S(1)}, bf16[8,128,128]{2,1,0:T(8,128)(2,1)S(1)}, bf16[128,128]{1,0:T(8,128)(2,1)S(1)}, bf16[128,128]{1,0:T(8...) custom-call(bf16[2,1024,128]{2,1,0:T(8,128)(2,1)} %bitcast.14, ...), custom_call_target="tpu_custom_call" | custom-call | tf_op jit(solution)/shard_map/pallas_call | solution.py:494
  3.1 3.1 %collective-permute-start = (bf16[128,128]{1,0:T(8,128)(2,1)S(1)}, bf16[128,128]{1,0:T(8,128)(2,1)S(1)}, u32[]{:S(2)}, u32[]{:S(2)}) collective-permute-start(bf16[128,128]{1,0:T(8,128)(2,1)S(1)} %get-tuple-element.34.first_own), channel_id=1, source_target_pairs={{8,10},{10,8},{12,14},{14,12},{0,2},{2,0},{4,6},{6,4},{9,11},{11,9... | collective-permute-start | bytes 98312 | tf_op jit(solution)/shard_map/ppermute | solution.py:37
  6.2 3.6 %collective-permute-start.1 = (bf16[128,128]{1,0:T(8,128)(2,1)S(1)}, bf16[128,128]{1,0:T(8,128)(2,1)S(1)}, u32[]{:S(2)}, u32[]{:S(2)}) collective-permute-start(bf16[128,128]{1,0:T(8,128)(2,1)S(1)} %get-tuple-element.35.second_own), channel_id=1, source_target_pairs={{10,12},{12,10},{14,0},{0,14},{2,4},{4,2},{6,8},{8,6},{11,13},{13,... | collective-permute-start | bytes 98312 | tf_op jit(solution)/shard_map/ppermute | solution.py:37
  9.7 3.0 %shard_map.78 = (bf16[8,512,128]{2,1,0:T(8,128)(2,1)S(1)}, f32[1024,128]{1,0:T(8,128)S(1)}, bf16[8,128,128]{2,1,0:T(8,128)(2,1)S(1)}, bf16[512,2304]{1,0:T(8,128)(2,1)S(1)}) custom-call(bf16[8,512,128]{2,1,0:T(8,128)(2,1)S(1)} %get-tuple-element.33.xt, f32[2,512,128]{2,1,0:T(8,128)S(1)} %get-tuple-element.38.bias, ...), custom_call_target="tpu_custom_call" | custom-call | tf_op jit(solution)/shard_map/pallas_call | solution.py:494
  12.7 0.0 collective-permute-done.first_got
  12.7 0.1 collective-permute-done.1.second_got
  12.8 0.4 %shard_map.77 = (bf16[3,128,128]{2,1,0:T(8,128)(2,1)S(1)}, bf16[128,128]{1,0:T(8,128)(2,1)S(1)}, bf16[128,128]{1,0:T(8,128)(2,1)S(1)}, bf16[3,256,128]{2,1,0:T(8,128)(2,1)S(1)}, f32[2,128,128]{2,1,0:T(8,128)S(1)}) custom-call(bf16[128,128]{1,0:T(8,128)(2,1)S(1)} %get-tuple-element.34.first_own, bf16[128,128]{1,0:T(8,128)(2,1)S(1)} %get-tuple-element.35.second_own, ...), custom_call_target="tpu_custom_call" | custom-call | tf_op jit(solution)/shard_map/pallas_call | solution.py:494
  13.2 1.0 %shard_map.79 = (bf16[9,128,128]{2,1,0:T(8,128)(2,1)S(1)}, f32[128,128]{1,0:T(8,128)S(1)}, bf16[512,128]{1,0:T(8,128)(2,1)S(1)}) custom-call(bf16[3,256,128]{2,1,0:T(8,128)(2,1)S(1)} %get-tuple-element.36.taps, bf16[512,2304]{1,0:T(8,128)(2,1)S(1)} %get-tuple-element.37.last_weights, f32[2,512,128]{2,1,0:T(8,128)S(1)} %get-tuple-element.38.bias, ...), custom_call_target="tpu_custom_call" | custom-call | tf_op jit(solution)/shard_map/pallas_call | solution.py:494
  14.3 1.6 %collective-permute-start.2 = (bf16[9,128,128]{2,1,0:T(8,128)(2,1)S(1)}, bf16[9,128,128]{2,1,0:T(8,128)(2,1)S(1)}, u32[]{:S(2)}, u32[]{:S(2)}) collective-permute-start(bf16[9,128,128]{2,1,0:T(8,128)(2,1)S(1)} %get-tuple-element.42.last), channel_id=1, source_target_pairs={{0,16},{16,0},{1,17},{17,1},{2,18},{18,2},{3,19},{19,3},{4,20},{20... | collective-permute-start | bytes 884744 | tf_op jit(solution)/shard_map/ppermute | solution.py:37
  15.8 0.5 %collective-permute-start.3 = (bf16[8,128,128]{2,1,0:T(8,128)(2,1)S(1)}, bf16[8,128,128]{2,1,0:T(8,128)(2,1)S(1)}, u32[]{:S(2)}, u32[]{:S(2)}) collective-permute-start(bf16[8,128,128]{2,1,0:T(8,128)(2,1)S(1)} %get-tuple-element.44), channel_id=1, source_target_pairs={{0,16},{16,0},{1,17},{17,1},{2,18},{18,2},{3,19},{19,3},{4,20},{20... | collective-permute-start | bytes 786440 | tf_op jit(solution)/shard_map/ppermute | solution.py:37
  16.4 1.5 %collective-permute-start.4 = (bf16[128,128]{1,0:T(8,128)(2,1)S(1)}, bf16[128,128]{1,0:T(8,128)(2,1)S(1)}, u32[]{:S(2)}, u32[]{:S(2)}) collective-permute-start(bf16[128,128]{1,0:T(8,128)(2,1)S(1)} %get-tuple-element.45), channel_id=1, source_target_pairs={{0,16},{16,0},{1,17},{17,1},{2,18},{18,2},{3,19},{19,3},{4,20},{20... | collective-permute-start | bytes 98312 | tf_op jit(solution)/shard_map/ppermute | solution.py:37
  17.8 1.0 %shard_map.80 = (f32[1024,128]{1,0:T(8,128)S(1)}, bf16[4096,128]{1,0:T(8,128)(2,1)S(1)}) custom-call(bf16[8,512,128]{2,1,0:T(8,128)(2,1)S(1)} %get-tuple-element.48.rough_gates, f32[1024,128]{1,0:T(8,128)S(1)} %get-tuple-element.49.rough_memory, bf16[512,128]{1,0:T(8,128)(2,1)S(1)} %get-tuple-element.50.edge_gates, f32[128,128]{1,0:T(8,128)S(1)} %get-tuple-element.51.edge_memory), custom_call_target="tpu_custom_call" | custom-call | tf_op jit(solution)/shard_map/pallas_call | solution.py:494
  18.9 9.9 %collective-permute-done.4.packet_edge = bf16[128,128]{1,0:T(8,128)(2,1)S(1)} collective-permute-done((bf16[128,128]{1,0:T(8,128)(2,1)S(1)}, bf16[128,128]{1,0:T(8,128)(2,1)S(1)}, u32[]{:S(2)}, u32[]{:S(2)}) %collective-permute-start.4) | collective-permute-done | bytes 32800 | tf_op jit(solution)/shard_map/ppermute | solution.py:37
  28.8 0.0 collective-permute-done.3.packet
  28.8 6.8 %shard_map.81 = (bf16[9,128,128]{2,1,0:T(8,128)(2,1)S(1)}, f32[1024,128]{1,0:T(8,128)S(1)}, bf16[8,512,128]{2,1,0:T(8,128)(2,1)S(1)}, f32[1024,128]{1,0:T(8,128)...) custom-call(bf16[8,512,128]{2,1,0:T(8,128)(2,1)S(1)} %get-tuple-element.33.xt, ...), custom_call_target="tpu_custom_call" | custom-call | tf_op jit(solution)/shard_map/pallas_call | solution.py:494
  35.6 0.0 collective-permute-done.2.packet
  35.6 5.1 %shard_map.82 = (bf16[2,2,4096,128]{3,2,1,0:T(8,128)(2,1)}, bf16[2,1024,128]{2,1,0:T(8,128)(2,1)}, f32[2,1024,128]{2,1,0:T(8,128)}) custom-call(bf16[8,512,128]{2,1,0:T(8,128)(2,1)S(1)} %get-tuple-element.33.xt, bf16[9,128,128]{2,1,0:T(8,128)(2,1)S(1)} %collective-permute-done.2.packet, ...), custom_call_target="tpu_custom_call", output_to_operand_aliasing={{0}: (10, {})} | custom-call | tf_op jit(solution)/shard_map/pallas_call | solution.py:494
Async XLA Ops:
  3.1 9.6 %collective-permute-start = (bf16[128,128]{1,0:T(8,128)(2,1)S(1)}, bf16[128,128]{1,0:T(8,128)(2,1)S(1)}, u32[]{:S(2)}, u32[]{:S(2)}) collective-permute-start(bf16[128,128]{1,0:T(8,128)(2,1)S(1)} %get-tuple-element.34.first_own), channel_id=1, source_target_pairs={{8,10},{10,8},{12,14},{14,12},{0,2},{2,0},{4,6},{6,4},{9,11},{11,9... | collective-permute-start | bytes 98312 | tf_op jit(solution)/shard_map/ppermute | solution.py:37
  6.2 6.6 %collective-permute-start.1 = (bf16[128,128]{1,0:T(8,128)(2,1)S(1)}, bf16[128,128]{1,0:T(8,128)(2,1)S(1)}, u32[]{:S(2)}, u32[]{:S(2)}) collective-permute-start(bf16[128,128]{1,0:T(8,128)(2,1)S(1)} %get-tuple-element.35.second_own), channel_id=1, source_target_pairs={{10,12},{12,10},{14,0},{0,14},{2,4},{4,2},{6,8},{8,6},{11,13},{13,... | collective-permute-start | bytes 98312 | tf_op jit(solution)/shard_map/ppermute | solution.py:37
  14.3 21.3 %collective-permute-start.2 = (bf16[9,128,128]{2,1,0:T(8,128)(2,1)S(1)}, bf16[9,128,128]{2,1,0:T(8,128)(2,1)S(1)}, u32[]{:S(2)}, u32[]{:S(2)}) collective-permute-start(bf16[9,128,128]{2,1,0:T(8,128)(2,1)S(1)} %get-tuple-element.42.last), channel_id=1, source_target_pairs={{0,16},{16,0},{1,17},{17,1},{2,18},{18,2},{3,19},{19,3},{4,20},{20... | collective-permute-start | bytes 884744 | tf_op jit(solution)/shard_map/ppermute | solution.py:37
  15.8 13.0 %collective-permute-start.3 = (bf16[8,128,128]{2,1,0:T(8,128)(2,1)S(1)}, bf16[8,128,128]{2,1,0:T(8,128)(2,1)S(1)}, u32[]{:S(2)}, u32[]{:S(2)}) collective-permute-start(bf16[8,128,128]{2,1,0:T(8,128)(2,1)S(1)} %get-tuple-element.44), channel_id=1, source_target_pairs={{0,16},{16,0},{1,17},{17,1},{2,18},{18,2},{3,19},{19,3},{4,20},{20... | collective-permute-start | bytes 786440 | tf_op jit(solution)/shard_map/ppermute | solution.py:37
  16.4 12.4 %collective-permute-start.4 = (bf16[128,128]{1,0:T(8,128)(2,1)S(1)}, bf16[128,128]{1,0:T(8,128)(2,1)S(1)}, u32[]{:S(2)}, u32[]{:S(2)}) collective-permute-start(bf16[128,128]{1,0:T(8,128)(2,1)S(1)} %get-tuple-element.45), channel_id=1, source_target_pairs={{0,16},{16,0},{1,17},{17,1},{2,18},{18,2},{3,19},{19,3},{4,20},{20... | collective-permute-start | bytes 98312 | tf_op jit(solution)/shard_map/ppermute | solution.py:37
